TPU v7x, 32 devices: a whole 2x2x4 slice. The times are simulated.
32 devices in a mesh: groups: 2 (over y), lon: 4 (over z), lat: 2 (over x), dp: 2 (over core).
Axes of the slice: x: 2, y: 2, z: 4, core: 2. Of those that a mesh axis runs over, the one named last changes fastest.
Arguments:
- inputs: bfloat16 [4, 128, 1024, 128], P(('groups', 'dp'), 'lat', 'lon'), parts along dimension 0, may hold values from -6 to 6
- cotangent: bfloat16 [4, 128, 1024, 128], P(('groups', 'dp'), 'lat', 'lon'), parts along dimension 0, may hold values from -6 to 6
- kernel_dw: bfloat16 [7, 7, 128], replicated, may hold values from -0.875 to 0.875
- bias_dw: float32 [128], replicated, may hold values from -3 to 3
- gain: float32 [128], replicated, may hold values from 0.1 to 1.9
- shift_ln: float32 [128], replicated, may hold values from -2 to 2
- w_in: bfloat16 [128, 256], replicated, may hold values from -0.5 to 0.5
- b_in: float32 [256], replicated, may hold values from -2 to 2
- w_out: bfloat16 [256, 128], replicated, may hold values from -0.375 to 0.375
- ocean_mask: int32 [2, 16], P('lat', 'lon'), may hold values from 0 to 1, as said below
Outputs:
- grad_inputs: bfloat16 [4, 128, 1024, 128], P(('groups', 'dp'), 'lat', 'lon'), parts along dimension 0
- grad_w_in: float32 [256, 256], P(('groups', 'dp')), parts along dimension 0
- grad_w_out: float32 [512, 128], P(('groups', 'dp')), parts along dimension 0
- grad_kernel: float32 [14, 7, 128], P('groups'), parts along dimension 0
- grad_bias_dw: float32 [256], P('groups'), parts along dimension 0
- grad_gain: float32 [256], P('groups'), parts along dimension 0
- grad_shift: float32 [256], P('groups'), parts along dimension 0
- grad_b_in: float32 [512], P('groups'), parts along dimension 0
There are 2 independent parts, one for each index of `groups`. A program takes and returns all parts, laid end to end along the dimension named above; an argument that names none is the same for every part. Nothing has to cross between parts.
Inputs may be any that keep to these rules, and one draw needn't show every extreme that they name: `ocean_mask`: every block of the northernmost block row (index 1) is ocean, and each aligned run of 4 blocks of a block row holds at least one ocean block.
All inputs are finite; a program needn't handle non-finite values.
Results may differ from a plain program's by a relative error of at most 0.0056.
Values may be sent and summed in bfloat16 or wider, within the bound.
A program may use at most 128 MiB of HBM per device.

v0:
```python
import math

import jax
import jax.numpy as jnp
from jax import lax
from jax.sharding import PartitionSpec as P

KS = 7


EPS = 1e-06
GELU_K = 0.7978845608
GELU_C = 0.044715


def padded(block, sides, width, periodic):
    for axis, dim in sides:
        count = lax.axis_size(axis)
        forward = [(i, i + 1) for i in range(count - 1)]
        if periodic:
            forward.append((count - 1, 0))
        backward = [(target, source) for source, target in forward]
        low = lax.ppermute(
            lax.slice_in_dim(block, block.shape[dim] - width, None, axis=dim), axis, forward
        )
        high = lax.ppermute(lax.slice_in_dim(block, 0, width, axis=dim), axis, backward)
        block = jnp.concatenate([low, block, high], axis=dim)
    return block


def partner(block, axis, stride):
    count = lax.axis_size(axis)
    route = []
    for low in range(count):
        high = low | 1 << stride
        if high != low and high < count:
            route += [(low, high), (high, low)]
    return lax.ppermute(block, axis, route)


def extend(field):
    half = KS // 2
    rows = field.shape[1]
    framed = padded(field, (("lat", 1),), half, False)
    mirror = field[:, rows - half :]
    for bit in range(lax.axis_size("lon").bit_length() - 1):
        mirror = partner(mirror, "lon", bit)
    band = mirror[:, ::-1, ::-1, :]
    northern = lax.axis_index("lat") == lax.axis_size("lat") - 1
    upper = jnp.where(northern, band, framed[:, rows + half :])
    framed = jnp.concatenate([framed[:, : rows + half], upper], 1)
    return padded(framed, (("lon", 2),), half, True)


def conv_valid(extended, kernel):
    return lax.conv_general_dilated(
        extended,
        kernel[:, :, None, :],
        (1, 1),
        "VALID",
        dimension_numbers=("NHWC", "HWIO", "NHWC"),
        feature_group_count=extended.shape[3],
        preferred_element_type=jnp.float32,
    )


def kernel_grad(extended, delta):
    out = lax.conv_general_dilated(
        extended[None],
        delta[:, :, None, :],
        (1, 1),
        "VALID",
        dimension_numbers=("NHWC", "HWIO", "NHWC"),
        feature_group_count=extended.shape[2],
        preferred_element_type=jnp.float32,
    )
    return out[0]


def cell_grads(ycells, gcells, maskval, gain, shift_ln, w_in, b_in, w_out):
    center = ycells - jnp.mean(ycells, -1, keepdims=True)
    rstd = lax.rsqrt(jnp.mean(center * center, -1, keepdims=True) + EPS)
    nhat = center * rstd
    normed = (nhat * gain + shift_ln).astype(jnp.bfloat16)
    pre = jnp.dot(normed, w_in, preferred_element_type=jnp.float32) + b_in
    tangent = jnp.tanh(GELU_K * (pre + GELU_C * pre * pre * pre))
    act = (0.5 * pre * (1.0 + tangent)).astype(jnp.bfloat16)
    outgrad = (gcells.astype(jnp.float32) * maskval).astype(jnp.bfloat16)
    g_out = lax.dot_general(
        act, outgrad, (((0,), (0,)), ((), ())), preferred_element_type=jnp.float32
    )
    dact = lax.dot_general(
        outgrad, w_out, (((1,), (1,)), ((), ())), preferred_element_type=jnp.float32
    )
    slope = 0.5 * (1.0 + tangent) + 0.5 * pre * (1.0 - tangent * tangent) * GELU_K * (
        1.0 + 3.0 * GELU_C * pre * pre
    )
    dpre = dact * slope
    dpre_b = dpre.astype(jnp.bfloat16)
    g_in = lax.dot_general(
        normed, dpre_b, (((0,), (0,)), ((), ())), preferred_element_type=jnp.float32
    )
    g_bin = jnp.sum(dpre, 0)
    dnorm = lax.dot_general(
        dpre_b, w_in, (((1,), (1,)), ((), ())), preferred_element_type=jnp.float32
    )
    g_gain = jnp.sum(dnorm * nhat, 0)
    g_shift = jnp.sum(dnorm, 0)
    dscaled = dnorm * gain
    delta = rstd * (
        dscaled
        - jnp.mean(dscaled, -1, keepdims=True)
        - nhat * jnp.mean(dscaled * nhat, -1, keepdims=True)
    )
    return (delta.astype(jnp.bfloat16), (g_in, g_bin, g_out, g_gain, g_shift))


def local(inputs, cotangent, kernel_dw, bias_dw, gain, shift_ln, w_in, b_in, w_out, ocean_mask):
    batch, rows, cols, chans = inputs.shape
    hidden = w_in.shape[1]
    half = KS // 2
    per_tile = cols // rows
    extended = extend(inputs)
    field_y = conv_valid(extended, kernel_dw) + bias_dw

    def to_blocks(field):
        parts = field.reshape(batch, rows, per_tile, rows, chans).transpose(0, 2, 1, 3, 4)
        return parts.reshape(batch * per_tile, rows * rows, chans)

    masks = jnp.tile(ocean_mask.reshape(-1), batch).astype(jnp.float32)
    totals = (
        jnp.zeros((chans, hidden), jnp.float32),
        jnp.zeros((hidden,), jnp.float32),
        jnp.zeros((hidden, chans), jnp.float32),
        jnp.zeros((chans,), jnp.float32),
        jnp.zeros((chans,), jnp.float32),
    )

    def step(carry, items):
        ycells, gcells, maskval = items
        delta, grads = cell_grads(ycells, gcells, maskval, gain, shift_ln, w_in, b_in, w_out)
        return (tuple((c + g for c, g in zip(carry, grads))), delta)

    totals, deltas = lax.scan(step, totals, (to_blocks(field_y), to_blocks(cotangent), masks))
    delta = (
        deltas.reshape(batch, per_tile, rows, rows, chans)
        .transpose(0, 2, 1, 3, 4)
        .reshape(batch, rows, cols, chans)
    )
    g_kernel = jnp.zeros((KS, KS, chans), jnp.float32)
    g_kernel = g_kernel + kernel_grad(extended[0], delta[0])
    g_bias = jnp.sum(delta.astype(jnp.float32), (0, 1, 2))
    spread = extend(delta)
    northern = lax.axis_index("lat") == lax.axis_size("lat") - 1
    fold_rows = spread[:, rows + half :]
    direct_part = jnp.concatenate(
        [spread[:, : rows + half], jnp.where(northern, jnp.zeros_like(fold_rows), fold_rows)], 1
    )
    direct = conv_valid(direct_part, kernel_dw[::-1, ::-1])
    fold_part = jnp.concatenate(
        [
            jnp.zeros_like(spread[:, rows - half : rows + half]),
            jnp.where(northern, fold_rows, jnp.zeros_like(fold_rows)),
        ],
        1,
    )
    fold = conv_valid(fold_part, kernel_dw)
    total = cotangent.astype(jnp.float32) + direct
    total = total.at[:, rows - half :].add(fold)
    grad_inputs = total.astype(jnp.bfloat16)
    g_in, g_bin, g_out, g_gain, g_shift = totals
    cells_all = (
        lax.axis_size("dp") * batch * lax.axis_size("lat") * rows * lax.axis_size("lon") * cols
    )
    scale = 1.0 / math.sqrt(cells_all)
    in_share = chans // lax.axis_size("dp")
    out_share = hidden // lax.axis_size("dp")
    summed = lax.psum((g_in, g_out, g_kernel, g_bias, g_gain, g_shift, g_bin), ("lon", "lat", "dp"))
    s_in, s_out, s_kernel, s_bias, s_gain, s_shift, s_bin = summed
    position = lax.axis_index("dp")
    s_in = lax.dynamic_slice_in_dim(s_in, position * in_share, in_share, 0)
    s_out = lax.dynamic_slice_in_dim(s_out, position * out_share, out_share, 0)
    return (
        grad_inputs,
        s_in * scale,
        s_out * scale,
        s_kernel * scale,
        s_bias * scale,
        s_gain * scale,
        s_shift * scale,
        s_bin * scale,
    )


def solution(mesh):
    placed = (
        P(("groups", "dp"), "lat", "lon", None),
        P(("groups", "dp"), "lat", "lon", None),
        P(),
        P(),
        P(),
        P(),
        P(),
        P(),
        P(),
        P("lat", "lon"),
    )
    return jax.shard_map(
        local,
        mesh=mesh,
        in_specs=placed,
        out_specs=(
            P(("groups", "dp"), "lat", "lon", None),
            P(("groups", "dp"), None),
            P(("groups", "dp"), None),
            P("groups", None, None),
            P("groups"),
            P("groups"),
            P("groups"),
            P("groups"),
        ),
        check_vma=False,
    )
```

profile of v0, /device:TPU:0, one launch (start us, length us, event | category | flops | bytes accessed | tf_op | source)
XLA Modules:
  0.0 606.1 jit_solution(1043596594227008258)
XLA Ops:
  7.2 7.8 %copy.54 = bf16[1,64,256,128]{3,0,2,1:T(2,128)(2,1)S(1)} copy(bf16[1,64,256,128]{3,2,1,0:T(8,128)(2,1)} %param.14) | data formatting | bytes 8388608 | tf_op args[0]
  15.0 3.3 copy-done
  19.1 3.1 collective-permute-start.1
  23.4 7.8 %collective-permute-done.1 = bf16[1,3,256,128]{3,0,2,1:T(2,128)(2,1)S(1)} collective-permute-done((bf16[1,3,256,128]{3,0,2,1:T(2,128)(2,1)S(1)}, bf16[1,3,256,128]{3,0,2,1:T(2,128)(2,1)S(1)}, u32[]{:S(2)}, u32[]{:S(2)}) %collective-permute-start.1) | collective-permute-done | bytes 196640 | tf_op jit(solution)/shard_map/ppermute | solution.py:38
  31.3 2.8 collective-permute-start.2
  34.0 3.4 collective-permute-start
  37.4 13.4 %collective-permute-done.2 = bf16[1,3,256,128]{3,0,2,1:T(2,128)(2,1)S(1)} collective-permute-done((bf16[1,3,256,128]{3,0,2,1:T(2,128)(2,1)S(1)}, bf16[1,3,256,128]{3,0,2,1:T(2,128)(2,1)S(1)}, u32[]{:S(2)}, u32[]{:S(2)}) %collective-permute-start.2) | collective-permute-done | bytes 196640 | tf_op jit(solution)/shard_map/ppermute | solution.py:38
  53.4 3.3 collective-permute-start.5
  57.4 5.5 copy.64
  62.9 41.8 %pad_maximum_fusion = bf16[1,70,262,128]{3,0,2,1:T(2,128)(2,1)S(1)} fusion(bf16[1,70,3,128]{3,0,2,1:T(2,128)(2,1)S(1)} %collective-permute-done.5, bf16[1,3,256,128]{3,0,2,1:T(2,128)(2,1)S(1)} %broadcast_select_fusion.4, bf16[1,64,256,128]{3,0,2,1:T(2,128)(2,1)} %copy-done, bf16[1,3,256,128]{3,0,2,1:T(2,128)(2,1)S(1)} %collective-permute-done, ...), kind=kLoop, calls=%fused_computation.47 | loop fusion | flops 9390080 | bytes 9390080 | tf_op jit(solution)/shard_map/concatenate | solution.py:27
  105.4 3.0 copy-done.3
  110.8 34.0 %select_add_fusion.1 = f32[64,8,33,128]{3,1,2,0:T(8,128)S(1)} fusion(f32[128]{0:T(128)S(1)} %copy-done.20, pred[8,33]{0,1:T(8,128)(4,1)S(1)} %copy-done.21, bf16[70,1,7,6,128]{4,2,3,0,1:T(8,128)(2,1)S(1)} %slice.80, bf16[70,1,8,33,128]{4,2,3,0,1:T(8,128)(2,1)S(1)} %copy.59, bf16[7,7,1,128]{3,1,0,2:T(8,128)(2,1)S(1)} %bitcast.144), kind=kOutput, calls=%fused_computation.48 | convolution fusion | flops 233041920 | bytes 14147592 | tf_op jit(solution)/shard_map/conv_general_dilated | solution.py:56
  148.2 4.9 copy.62
  153.1 4.2 copy.63
  157.3 98.5 %while.22 = (s32[]{:T(128)}, f32[128,256]{1,0:T(8,128)S(1)}, f32[256]{0:T(256)S(1)}, f32[256,128]{1,0:T(8,128)S(1)}, f32[128]{0:T(128)S(1)}, /*index=5*/f32[128]...) while((s32[]{:T(128)}, f32[128,256]{1,0:T(8,128)S(1)}, ...), condition=%wide.region_8.9_spmd.clone, body=%wide.region_0.8_spmd.clone.sunk | while | flops 1393168896 | bytes 81850672 | solution.py:144
  160.5 2.7 multiply_reduce_fusion.6
  163.2 3.9 convolution_add_fusion.4
  169.8 3.9 fusion.103
  178.1 4.1 fusion.106
  185.0 2.7 multiply_reduce_fusion.6
  187.7 3.9 convolution_add_fusion.4
  191.7 2.6 fusion.104
  194.3 3.9 fusion.103
  202.6 4.1 fusion.106
  209.6 2.7 multiply_reduce_fusion.6
  212.2 3.9 convolution_add_fusion.4
  216.2 2.6 fusion.104
  218.8 3.9 fusion.103
  227.1 4.1 fusion.106
  234.1 2.7 multiply_reduce_fusion.6
  236.7 3.9 convolution_add_fusion.4
  243.3 3.9 fusion.103
  251.6 4.1 fusion.106
  255.8 4.5 convert_reduce_fusion
  262.1 3.3 collective-permute-start.6
  265.4 90.3 %fusion.29 = f32[1,7,7,128]{3,0,2,1:T(1,128)S(1)} fusion(bf16[1,70,262,128]{3,0,2,1:T(2,128)(2,1)} %copy-done.3, bf16[64,256,1,128]{3,1,0,2:T(8,128)(2,1)S(1)} %bitcast.128), kind=kOutput, calls=%fused_computation.51 | convolution fusion | flops 205520896 | bytes 8914432 | tf_op jit(solution)/shard_map/conv_general_dilated | solution.py:68
  355.8 57.7 %all-reduce = (f32[7,7,128]{2,1,0:T(8,128)S(1)}, f32[128]{0:T(128)S(1)}, f32[128]{0:T(128)S(1)}, f32[128]{0:T(128)S(1)}, f32[256]{0:T(256)S(1)}) all-reduce(f32[7,7,128]{2,1,0:T(8,128)S(1)} %bitcast.143, f32[128]{0:T(128)S(1)} %convert_reduce_fusion, ...), channel_id=1, replica_groups=mesh['groups'=2,'lon'=4,'lat'=2,'dp'=2] {'lon','lat','dp'}, use_global_device_ids=true, to_apply=%region_11.12 | all-reduce | flops 6912 | bytes 55296 | tf_op jit(solution)/shard_map/psum | solution.py:178
  417.3 91.0 %all-reduce.4.cloned.1.call-done = (f32[128,256]{1,0:T(8,128)}, f32[256,128]{1,0:T(8,128)}) async-done(((f32[128,256]{1,0:T(8,128)}, f32[256,128]{1,0:T(8,128)}), (f32[128,256]{1,0:T(8,128)}, f32[256,128]{1,0:T(8,128)})) %all-reduce.4.cloned.1.call-update) | async-done | bytes 262160 | tf_op jit(solution)/shard_map/psum | solution.py:178
  511.7 3.0 collective-permute-start.10
  519.2 5.8 pad_maximum_fusion.1
  529.0 2.7 maximum_bitcast_fusion
  534.1 33.5 %broadcast_select_fusion.2 = f32[64,8,33,128]{3,1,2,0:T(8,128)S(1)} fusion(pred[8,33]{0,1:T(8,128)(4,1)S(1)} %copy-done.22, bf16[70,1,7,6,128]{4,2,3,0,1:T(8,128)(2,1)S(1)} %slice.85, bf16[70,1,8,33,128]{4,2,3,0,1:T(8,128)(2,1)S(1)} %copy.72, bf16[7,7,1,128]{3,1,0,2:T(8,128)(2,1)S(1)} %bitcast.146), kind=kOutput, calls=%fused_computation.69 | convolution fusion | flops 230879232 | bytes 14147080 | tf_op jit(solution)/shard_map/conv_general_dilated | solution.py:56
  567.7 4.9 copy.74
  572.6 6.2 %fusion.28 = f32[1,64,256,128]{3,1,2,0:T(8,128)S(1)} fusion(f32[64,1,264,128]{3,0,2,1:T(8,128)} %bitcast.133, bf16[1,64,256,128]{3,2,1,0:T(8,128)(2,1)S(1)} %copy-done.5), kind=kLoop, calls=%fused_computation.50 | loop fusion | flops 4194304 | bytes 20971520 | tf_op jit(solution)/shard_map/add | solution.py:168
  578.8 3.3 copy-done.4
  582.2 7.6 %scatter-add.4 = f32[1,64,256,128]{3,1,2,0:T(8,128)} dynamic-update-slice(f32[1,64,256,128]{3,1,2,0:T(8,128)} %copy-done.4, f32[1,3,256,128]{3,1,2,0:T(4,128)S(1)} %fusion.51, s32[]{:T(128)} %constant.89.clone.1, s32[]{:T(128)} %constant.94.clone.1, s32[]{:T(128)} %constant.89.clone.1, s32[]{:T(128)} %constant.89.clone.1) | dynamic-update-slice | bytes 786436 | tf_op jit(solution)/shard_map/scatter-add | solution.py:169
  589.8 4.5 convert_element_type.43
  594.3 4.7 copy.82
  (172 shorter events, 65.2 us)
Async XLA Ops:
  7.2 501.1 %all-reduce.4.cloned.1.call-start = ((), (), s32[]{:S(2)}) async-start(), calls=%async_computation | async-start | bytes 524288 | tf_op jit(solution)/shard_map/psum | solution.py:178
  15.0 3.3 copy-start
  19.1 12.2 %collective-permute-start.1 = (bf16[1,3,256,128]{3,0,2,1:T(2,128)(2,1)S(1)}, bf16[1,3,256,128]{3,0,2,1:T(2,128)(2,1)S(1)}, u32[]{:S(2)}, u32[]{:S(2)}) collective-permute-start(bf16[1,3,256,128]{3,0,2,1:T(2,128)(2,1)S(1)} %get-tuple-element.224), channel_id=1, source_target_pairs={{0,4},{4,0},{8,12},{12,8},{1,5},{5,1},{9,13},{13,9},{2,6},{6,2},{1... | collective-permute-start | bytes 589832 | tf_op jit(solution)/shard_map/ppermute | solution.py:38
  22.1 15.3 %collective-permute-start.3 = (bf16[1,3,256,128]{3,0,2,1:T(2,128)(2,1)S(1)}, bf16[1,3,256,128]{3,0,2,1:T(2,128)(2,1)S(1)}, u32[]{:S(2)}, u32[]{:S(2)}) collective-permute-start(bf16[1,3,256,128]{3,0,2,1:T(2,128)(2,1)S(1)} %get-tuple-element.225), channel_id=1, source_target_pairs={{2,0},{3,1},{6,4},{7,5},{10,8},{11,9},{14,12},{15,13},{18,16},{19,... | collective-permute-start | bytes 589832 | tf_op jit(solution)/shard_map/ppermute | solution.py:26
  31.3 19.6 %collective-permute-start.2 = (bf16[1,3,256,128]{3,0,2,1:T(2,128)(2,1)S(1)}, bf16[1,3,256,128]{3,0,2,1:T(2,128)(2,1)S(1)}, u32[]{:S(2)}, u32[]{:S(2)}) collective-permute-start(bf16[1,3,256,128]{3,0,2,1:T(2,128)(2,1)S(1)} %collective-permute-done.1), channel_id=1, source_target_pairs={{0,8},{8,0},{4,12},{12,4},{1,9},{9,1},{5,13},{13,5},{2,10},{10,2},... | collective-permute-start | bytes 589832 | tf_op jit(solution)/shard_map/ppermute | solution.py:38
  34.0 17.5 %collective-permute-start = (bf16[1,3,256,128]{3,0,2,1:T(2,128)(2,1)S(1)}, bf16[1,3,256,128]{3,0,2,1:T(2,128)(2,1)S(1)}, u32[]{:S(2)}, u32[]{:S(2)}) collective-permute-start(bf16[1,3,256,128]{3,0,2,1:T(2,128)(2,1)S(1)} %get-tuple-element.224), channel_id=1, source_target_pairs={{0,2},{1,3},{4,6},{5,7},{8,10},{9,11},{12,14},{13,15},{16,18},{17,... | collective-permute-start | bytes 589832 | tf_op jit(solution)/shard_map/ppermute | solution.py:23
  51.5 5.2 copy-start.19
  51.5 5.2 copy-start.15
  52.8 10.1 %collective-permute-start.4 = (bf16[1,70,3,128]{3,0,2,1:T(2,128)(2,1)S(1)}, bf16[1,70,3,128]{3,0,2,1:T(2,128)(2,1)S(1)}, u32[]{:S(2)}, u32[]{:S(2)}) collective-permute-start(bf16[1,70,3,128]{3,0,2,1:T(2,128)(2,1)S(1)} %get-tuple-element.222), channel_id=1, source_target_pairs={{0,4},{4,8},{8,12},{12,0},{1,5},{5,9},{9,13},{13,1},{2,6},{6,10},{... | collective-permute-start | bytes 161288 | tf_op jit(solution)/shard_map/ppermute | solution.py:23
  53.4 9.5 %collective-permute-start.5 = (bf16[1,70,3,128]{3,0,2,1:T(2,128)(2,1)S(1)}, bf16[1,70,3,128]{3,0,2,1:T(2,128)(2,1)S(1)}, u32[]{:S(2)}, u32[]{:S(2)}) collective-permute-start(bf16[1,70,3,128]{3,0,2,1:T(2,128)(2,1)S(1)} %get-tuple-element.223), channel_id=1, source_target_pairs={{4,0},{8,4},{12,8},{0,12},{5,1},{9,5},{13,9},{1,13},{6,2},{10,6},{... | collective-permute-start | bytes 161288 | tf_op jit(solution)/shard_map/ppermute | solution.py:26
  104.7 3.7 copy-start.3
  109.9 0.9 copy-start.20
  109.9 0.9 copy-start.21
  153.1 4.2 copy-start.9
  153.1 4.2 copy-start.11
  153.1 4.2 copy-start.12
  153.1 4.2 copy-start.14
  153.1 4.2 copy-start.18
  160.5 6.6 %copy-start.8 = (bf16[4,4096,128]{2,1,0:T(8,128)(2,1)S(1)}, bf16[4,4096,128]{2,1,0:T(8,128)(2,1)}, u32[]{:S(2)}) copy-start(bf16[4,4096,128]{2,1,0:T(8,128)(2,1)} %get-tuple-element.391) | copy-start | bytes 12582916 | tf_op jit(solution)/shard_map/while
  167.1 6.6 %slice-start = ((s8[8388608]{0:T(1024)(128)(4,1)}), s8[4194304]{0:T(1024)(128)(4,1)S(1)}, s32[]{:S(2)}) async-start(s8[8388608]{0:T(1024)(128)(4,1)} %bitcast.125), calls=%async_computation.1 | async-start | bytes 8388608 | tf_op jit(solution)/shard_map/while
  169.8 4.0 slice-start.1
  185.0 6.6 %copy-start.8 = (bf16[4,4096,128]{2,1,0:T(8,128)(2,1)S(1)}, bf16[4,4096,128]{2,1,0:T(8,128)(2,1)}, u32[]{:S(2)}) copy-start(bf16[4,4096,128]{2,1,0:T(8,128)(2,1)} %get-tuple-element.391) | copy-start | bytes 12582916 | tf_op jit(solution)/shard_map/while
  191.6 6.6 %slice-start = ((s8[8388608]{0:T(1024)(128)(4,1)}), s8[4194304]{0:T(1024)(128)(4,1)S(1)}, s32[]{:S(2)}) async-start(s8[8388608]{0:T(1024)(128)(4,1)} %bitcast.125), calls=%async_computation.1 | async-start | bytes 8388608 | tf_op jit(solution)/shard_map/while
  194.3 4.0 slice-start.1
  209.5 6.6 %copy-start.8 = (bf16[4,4096,128]{2,1,0:T(8,128)(2,1)S(1)}, bf16[4,4096,128]{2,1,0:T(8,128)(2,1)}, u32[]{:S(2)}) copy-start(bf16[4,4096,128]{2,1,0:T(8,128)(2,1)} %get-tuple-element.391) | copy-start | bytes 12582916 | tf_op jit(solution)/shard_map/while
  216.2 6.6 %slice-start = ((s8[8388608]{0:T(1024)(128)(4,1)}), s8[4194304]{0:T(1024)(128)(4,1)S(1)}, s32[]{:S(2)}) async-start(s8[8388608]{0:T(1024)(128)(4,1)} %bitcast.125), calls=%async_computation.1 | async-start | bytes 8388608 | tf_op jit(solution)/shard_map/while
  218.8 4.0 slice-start.1
  234.1 6.6 %copy-start.8 = (bf16[4,4096,128]{2,1,0:T(8,128)(2,1)S(1)}, bf16[4,4096,128]{2,1,0:T(8,128)(2,1)}, u32[]{:S(2)}) copy-start(bf16[4,4096,128]{2,1,0:T(8,128)(2,1)} %get-tuple-element.391) | copy-start | bytes 12582916 | tf_op jit(solution)/shard_map/while
  240.7 6.6 %slice-start = ((s8[8388608]{0:T(1024)(128)(4,1)}), s8[4194304]{0:T(1024)(128)(4,1)S(1)}, s32[]{:S(2)}) async-start(s8[8388608]{0:T(1024)(128)(4,1)} %bitcast.125), calls=%async_computation.1 | async-start | bytes 8388608 | tf_op jit(solution)/shard_map/while
  243.3 4.0 slice-start.1
  255.8 5.9 copy-start.7
  255.8 5.9 copy-start.10
  255.8 4.5 copy-start.6
  261.7 94.0 %copy-start.1 = (bf16[1,64,4,64,128]{4,3,2,1,0:T(8,128)(2,1)}, bf16[1,64,4,64,128]{4,3,2,1,0:T(8,128)(2,1)S(1)}, u32[]{:S(2)}) copy-start(bf16[1,64,4,64,128]{4,3,2,1,0:T(8,128)(2,1)S(1)} %copy.65) | copy-start | bytes 12582916
  262.1 154.7 %collective-permute-start.7 = (bf16[1,3,256,128]{3,0,2,1:T(2,128)(2,1)S(1)}, bf16[1,3,256,128]{3,0,2,1:T(2,128)(2,1)S(1)}, u32[]{:S(2)}, u32[]{:S(2)}) collective-permute-start(bf16[1,3,256,128]{3,0,2,1:T(2,128)(2,1)S(1)} %copy.87), channel_id=1, source_target_pairs={{0,4},{4,0},{8,12},{12,8},{1,5},{5,1},{9,13},{13,9},{2,6},{6,2},{1... | collective-permute-start | bytes 589832 | tf_op jit(solution)/shard_map/ppermute | solution.py:38
  262.1 247.8 %collective-permute-start.6 = (bf16[1,3,256,128]{3,0,2,1:T(2,128)(2,1)S(1)}, bf16[1,3,256,128]{3,0,2,1:T(2,128)(2,1)S(1)}, u32[]{:S(2)}, u32[]{:S(2)}) collective-permute-start(bf16[1,3,256,128]{3,0,2,1:T(2,128)(2,1)S(1)} %copy.87), channel_id=1, source_target_pairs={{0,2},{1,3},{4,6},{5,7},{8,10},{9,11},{12,14},{13,15},{16,18},{17,... | collective-permute-start | bytes 589832 | tf_op jit(solution)/shard_map/ppermute | solution.py:23
  414.9 95.1 %collective-permute-start.9 = (bf16[1,3,256,128]{3,0,2,1:T(2,128)(2,1)S(1)}, bf16[1,3,256,128]{3,0,2,1:T(2,128)(2,1)S(1)}, u32[]{:S(2)}, u32[]{:S(2)}) collective-permute-start(bf16[1,3,256,128]{3,0,2,1:T(2,128)(2,1)S(1)} %copy.88), channel_id=1, source_target_pairs={{2,0},{3,1},{6,4},{7,5},{10,8},{11,9},{14,12},{15,13},{18,16},{19,... | collective-permute-start | bytes 589832 | tf_op jit(solution)/shard_map/ppermute | solution.py:26
  416.7 93.2 %collective-permute-start.8 = (bf16[1,3,256,128]{3,0,2,1:T(2,128)(2,1)S(1)}, bf16[1,3,256,128]{3,0,2,1:T(2,128)(2,1)S(1)}, u32[]{:S(2)}, u32[]{:S(2)}) collective-permute-start(bf16[1,3,256,128]{3,0,2,1:T(2,128)(2,1)S(1)} %collective-permute-done.7), channel_id=1, source_target_pairs={{0,8},{8,0},{4,12},{12,4},{1,9},{9,1},{5,13},{13,5},{2,10},{10,2},... | collective-permute-start | bytes 589832 | tf_op jit(solution)/shard_map/ppermute | solution.py:38
  508.3 7.3 %copy-start.13 = (f32[256,128]{1,0:T(8,128)S(1)}, f32[256,128]{1,0:T(8,128)}, u32[]{:S(2)}) copy-start(f32[256,128]{1,0:T(8,128)} %get-tuple-element.212) | copy-start | bytes 393220
  508.3 10.9 %copy-start.2 = (bf16[1,64,4,64,128]{4,3,2,1,0:T(8,128)(2,1)S(1)}, bf16[1,64,4,64,128]{4,3,2,1,0:T(8,128)(2,1)}, u32[]{:S(2)}) copy-start(bf16[1,64,4,64,128]{4,3,2,1,0:T(8,128)(2,1)} %copy-done.1) | copy-start | bytes 12582916
  511.7 6.9 %collective-permute-start.10 = (bf16[1,70,3,128]{3,2,1,0:T(4,128)(2,1)S(1)}, bf16[1,70,3,128]{3,2,1,0:T(4,128)(2,1)S(1)}, u32[]{:S(2)}, u32[]{:S(2)}) collective-permute-start(bf16[1,70,3,128]{3,2,1,0:T(4,128)(2,1)S(1)} %get-tuple-element.226), channel_id=1, source_target_pairs={{0,4},{4,8},{8,12},{12,0},{1,5},{5,9},{9,13},{13,1},{2,6},{6,10},{... | collective-permute-start | bytes 161288 | tf_op jit(solution)/shard_map/ppermute | solution.py:23
  514.7 4.5 collective-permute-start.11
  527.3 0.7 copy-start.16
  527.3 0.7 copy-start.22
  533.2 0.9 copy-start.17
  567.7 4.9 copy-start.5
  578.8 3.3 copy-start.4
Sparse Core Ops, SparseCore 0:
  416.3 91.9 all-reduce.3
where the time goes:
time: 611 us; the launch traced here: 606 us
  matrix products  218 us (36%)
  waiting for transfers between devices  115 us (19%)
  other arithmetic  110 us (18%)
  local copies, waits for them, and re-layouts  66.8 us (11%)
  blocking collectives  57.7 us (9%)
  starting transfers between devices  23 us (4%)
  between operations  14.9 us (2%)
    psum x1, waiting for transfers between devices, local(): lax.psum((g_in, g_out, g_kernel, g_bias, g_gain, g_shift, g_bin), ('lon',...  91 us
    conv_general_dilated x1, matrix products, kernel_grad(): lax.conv_general_dilated(extended[None], delta[:, :, None, :], (1, 1), 'V...  90.3 us
    conv_general_dilated x3, matrix products, conv_valid(): lax.conv_general_dilated(extended, kernel[:, :, None, :], (1, 1), 'VALID'...  68.3 us
    psum x1, blocking collectives, local(): lax.psum((g_in, g_out, g_kernel, g_bias, g_gain, g_shift, g_bin), ('lon',...  57.7 us
    concatenate x2, other arithmetic, padded(): block = jnp.concatenate([low, block, high], axis=dim)  47.6 us
    unnamed x52, local copies, waits for them, and re-layouts  25.1 us
    ppermute x4, waiting for transfers between devices, partner(): return lax.ppermute(block, axis, route)  21.3 us
    dynamic_update_slice x4, other arithmetic, local(): lax.scan(step, totals, (to_blocks(field_y), to_blocks(cotangent), masks))  16.5 us
  transfers between devices with their start and end apart: 13, of which 5 were waited for; matrix products, arithmetic and copies ran while one was open for 17% of the time, Pallas kernels for 0%

commit v1 on v0

v1 whole, which is shorter than its diff:
```python
import math

import jax
import jax.numpy as jnp
from jax import lax
from jax.experimental import pallas as pl
from jax.experimental.pallas import tpu as pltpu
from jax.sharding import PartitionSpec as P

KS = 7
HALF = 3
EPS = 1e-06
GELU_K = 0.7978845608
GELU_C = 0.044715
OFF = 8
ROWS_OUT = 8
COLS_OUT = 32
CELL_ROWS = 2
F32 = jnp.float32
BF16 = jnp.bfloat16


def load_extended(ext, tile, south, north, west, east):
    rows, cols, _ = tile.shape

    def fill(r, carry):
        ext[r + HALF, OFF : OFF + cols, :] = tile[r].astype(F32)
        return carry

    lax.fori_loop(0, rows, fill, 0)
    for m in range(HALF):
        ext[m, OFF : OFF + cols, :] = south[m].astype(F32)
        ext[rows + HALF + m, OFF : OFF + cols, :] = north[m].astype(F32)

    def sides(r, carry):
        ext[r, OFF - HALF : OFF, :] = west[r].astype(F32)
        ext[r, OFF + cols : OFF + cols + HALF, :] = east[r].astype(F32)
        return carry

    lax.fori_loop(0, rows + 2 * HALF, sides, 0)


def conv_steps(ext, taps, rows, cols, flip, finish):
    chunks = cols // COLS_OUT

    def step(i, carry):
        r0 = (i // chunks) * ROWS_OUT
        c0 = pl.multiple_of((i % chunks) * COLS_OUT, COLS_OUT)
        acc = [None] * ROWS_OUT
        for rho in range(ROWS_OUT + KS - 1):
            for b in range(KS):
                v = ext[r0 + rho, pl.ds(c0 + (OFF - HALF + b), COLS_OUT), :]
                v = v.reshape(COLS_OUT // 8, 8, v.shape[-1])
                for a in range(KS):
                    out = rho - a
                    if 0 <= out < ROWS_OUT:
                        t = a * KS + b
                        k = taps[KS * KS - 1 - t if flip else t]
                        term = v * k[None]
                        acc[out] = term if acc[out] is None else acc[out] + term
            if rho >= KS - 1:
                out = rho - (KS - 1)
                finish(r0 + out, c0, acc[out].reshape(COLS_OUT, acc[out].shape[-1]))
        return carry

    lax.fori_loop(0, (rows // ROWS_OUT) * chunks, step, 0)


def partial_sum(x):
    return jnp.sum(x.reshape(x.shape[0] // 8, 8, x.shape[1]), axis=0)


def cells_kernel(
    tile, south, north, west, east, cot, mask, taps, bias, gain, shift, w_in, w_in_t, b_in, w_out_t,
    dy, g_in, g_out, g_chan, g_bin,
    ext, y, s_chan, s_bin,
):
    rows, cols, chans = tile.shape
    hidden = w_in.shape[1]
    load_extended(ext, tile, south, north, west, east)
    bias_row = bias[...]

    def finish(r, c0, acc):
        y[r, pl.ds(c0, COLS_OUT), :] = acc + bias_row

    conv_steps(ext, taps, rows, cols, False, finish)
    g_in[...] = jnp.zeros_like(g_in)
    g_out[...] = jnp.zeros_like(g_out)
    s_chan[...] = jnp.zeros_like(s_chan)
    s_bin[...] = jnp.zeros_like(s_bin)
    count = CELL_ROWS * cols
    inv = 1.0 / chans

    def step(i, carry):
        r0 = i * CELL_ROWS
        yc = y[pl.ds(r0, CELL_ROWS)].reshape(count, chans)
        center = yc - jnp.sum(yc, -1, keepdims=True) * inv
        rstd = lax.rsqrt(jnp.sum(center * center, -1, keepdims=True) * inv + EPS)
        nhat = center * rstd
        normed = (nhat * gain[...] + shift[...]).astype(BF16)
        pre = jnp.dot(normed, w_in[...], preferred_element_type=F32) + b_in[...]
        square = pre * pre
        t = jnp.tanh(pre * (GELU_K + (GELU_K * GELU_C) * square))
        h = 0.5 + 0.5 * t
        act = pre * h
        slope = h + act * (1.0 - h) * (2.0 * GELU_K + (6.0 * GELU_K * GELU_C) * square)
        og = (cot[pl.ds(r0, CELL_ROWS)] * mask[...][None]).reshape(count, chans)
        g_out[...] += lax.dot_general(
            act.astype(BF16), og, (((0,), (0,)), ((), ())), preferred_element_type=F32
        )
        dpre = jnp.dot(og, w_out_t[...], preferred_element_type=F32) * slope
        dpre_b = dpre.astype(BF16)
        s_bin[...] += partial_sum(dpre)
        g_in[...] += lax.dot_general(
            normed, dpre_b, (((0,), (0,)), ((), ())), preferred_element_type=F32
        )
        dnorm = jnp.dot(dpre_b, w_in_t[...], preferred_element_type=F32)
        s_chan[0] += partial_sum(dnorm * nhat)
        s_chan[1] += partial_sum(dnorm)
        dn = dnorm * gain[...]
        m1 = jnp.sum(dn, -1, keepdims=True) * inv
        m2 = jnp.sum(dn * nhat, -1, keepdims=True) * inv
        delta = (rstd * (dn - m1 - nhat * m2)).astype(BF16)
        s_chan[2] += partial_sum(delta.astype(F32))
        dy[pl.ds(r0, CELL_ROWS)] = delta.reshape(CELL_ROWS, cols, chans)
        return carry

    lax.fori_loop(0, rows // CELL_ROWS, step, 0)
    for q in range(3):
        g_chan[q : q + 1, :] = jnp.sum(s_chan[q], axis=0, keepdims=True)
    g_bin[...] = jnp.sum(s_bin[...], axis=0, keepdims=True)


def taps_kernel(tile, south, north, west, east, dy, g_taps, ext, dyf):
    rows, cols, chans = tile.shape
    load_extended(ext, tile, south, north, west, east)
    edge = jnp.zeros((cols, chans), F32)
    for m in range(KS - 1):
        dyf[m] = edge
        dyf[rows + KS - 1 + m] = edge

    def fill(r, carry):
        dyf[r + KS - 1] = dy[r].astype(F32)
        return carry

    lax.fori_loop(0, rows, fill, 0)
    for first, last in ((0, 4), (4, KS)):

        def row_step(rho, acc):
            def col_step(j, acc):
                acc = list(acc)
                for sub in range(4):
                    c0 = pl.multiple_of(j * 32 + sub * 8, 8)
                    d = [dyf[rho + (KS - 1) - a, pl.ds(c0, 8), :] for a in range(first, last)]
                    for b in range(KS):
                        v = ext[rho, pl.ds(c0 + (OFF - HALF + b), 8), :]
                        for q in range(last - first):
                            at = q * KS + b
                            acc[at] = acc[at] + v * d[q]
                return tuple(acc)

            return lax.fori_loop(0, cols // 32, col_step, acc)

        zero = jnp.zeros((8, chans), F32)
        acc = lax.fori_loop(0, rows + KS - 1, row_step, (zero,) * (KS * (last - first)))
        for n, value in enumerate(acc):
            at = first * KS + n
            g_taps[at : at + 1, :] = jnp.sum(value, axis=0, keepdims=True)


def input_kernel(tile, south, north, west, east, cot, taps, is_north, out, ext, fold, total):
    rows, cols, chans = tile.shape
    load_extended(ext, tile, south, north, west, east)
    flag = is_north[0]
    for m in range(HALF):
        row = ext[rows + HALF + m]
        fold[m] = row * flag
        ext[rows + HALF + m] = row * (1.0 - flag)

    def finish(r, c0, acc):
        summed = acc + cot[r, pl.ds(c0, COLS_OUT), :].astype(F32)
        out[r, pl.ds(c0, COLS_OUT), :] = summed.astype(BF16)

        @pl.when(r >= rows - HALF)
        def _():
            total[r - (rows - HALF), pl.ds(c0, COLS_OUT), :] = summed

    conv_steps(ext, taps, rows, cols, True, finish)

    def fold_step(i, carry):
        c0 = pl.multiple_of(i * COLS_OUT, COLS_OUT)
        for m in range(HALF):
            acc = total[m, pl.ds(c0, COLS_OUT), :].reshape(COLS_OUT // 8, 8, chans)
            for n in range(m + 1):
                a = KS - 1 - m + n
                for b in range(KS):
                    v = fold[n, pl.ds(c0 + (OFF - HALF + b), COLS_OUT), :]
                    acc = acc + v.reshape(COLS_OUT // 8, 8, chans) * taps[a * KS + b][None]
            out[rows - HALF + m, pl.ds(c0, COLS_OUT), :] = acc.reshape(COLS_OUT, chans).astype(BF16)
        return carry

    lax.fori_loop(0, cols // COLS_OUT, fold_step, 0)


def halo(tile):
    rows, cols, _ = tile.shape
    lats, lons = lax.axis_size("lat"), lax.axis_size("lon")
    up = [(i, i + 1) for i in range(lats - 1)]
    down = [(i + 1, i) for i in range(lats - 1)]
    south = lax.ppermute(tile[rows - HALF :], "lat", up)
    above = lax.ppermute(tile[:HALF], "lat", down)
    mirror = lax.ppermute(tile[rows - HALF :], "lon", [(i, lons - 1 - i) for i in range(lons)])
    northern = lax.axis_index("lat") == lats - 1
    north = jnp.where(northern, mirror[::-1, ::-1, :], above)
    left = jnp.concatenate([south[:, :HALF], tile[:, :HALF], north[:, :HALF]], 0)
    right = jnp.concatenate([south[:, cols - HALF :], tile[:, cols - HALF :], north[:, cols - HALF :]], 0)
    west = lax.ppermute(right, "lon", [(i, (i + 1) % lons) for i in range(lons)])
    east = lax.ppermute(left, "lon", [((i + 1) % lons, i) for i in range(lons)])
    return south, north, west, east


def call(kernel, out_shape, scratch, flops, *args, scalars=0):
    vmem = pl.BlockSpec(memory_space=pltpu.VMEM)
    smem = pl.BlockSpec(memory_space=pltpu.SMEM)
    return pl.pallas_call(
        kernel,
        out_shape=out_shape,
        in_specs=[vmem] * (len(args) - scalars) + [smem] * scalars,
        out_specs=jax.tree.map(lambda _: vmem, out_shape),
        scratch_shapes=scratch,
        compiler_params=pltpu.CompilerParams(vmem_limit_bytes=56 * 1024 * 1024),
        cost_estimate=pl.CostEstimate(flops=flops, bytes_accessed=12 << 20, transcendentals=0),
    )(*args)


def local(inputs, cotangent, kernel_dw, bias_dw, gain, shift_ln, w_in, b_in, w_out, ocean_mask):
    batch, rows, cols, chans = inputs.shape
    hidden = w_in.shape[1]
    shape = jax.ShapeDtypeStruct
    taps = jnp.broadcast_to(kernel_dw.astype(F32).reshape(KS * KS, 1, chans), (KS * KS, 8, chans))
    blocks = ocean_mask.reshape(-1)
    mask = jnp.broadcast_to(
        jnp.repeat(blocks, cols // blocks.shape[0])[:, None], (cols, chans)
    ).astype(BF16)
    ext_shape = pltpu.VMEM((rows + 2 * HALF, cols + 2 * OFF, chans), F32)
    northern = lax.axis_index("lat") == lax.axis_size("lat") - 1
    is_north = jnp.where(northern, 1.0, 0.0).astype(F32).reshape(1)
    work = 2 * KS * KS * rows * cols * chans * 128
    sums, grads = None, []
    for n in range(batch):
        tile, cot = inputs[n], cotangent[n]
        frame = halo(tile)
        dy, g_in, g_out, g_chan, g_bin = call(
            cells_kernel,
            (
                shape(tile.shape, BF16),
                shape((chans, hidden), F32),
                shape((hidden, chans), F32),
                shape((3, chans), F32),
                shape((1, hidden), F32),
            ),
            [
                ext_shape,
                pltpu.VMEM((rows, cols, chans), F32),
                pltpu.VMEM((3, 8, chans), F32),
                pltpu.VMEM((8, hidden), F32),
            ],
            work,
            tile, *frame, cot, mask, taps, bias_dw[None], gain[None], shift_ln[None],
            w_in, w_in.T, b_in[None], w_out.T,
        )
        g_taps = call(
            taps_kernel,
            shape((KS * KS, chans), F32),
            [ext_shape, pltpu.VMEM((rows + 2 * (KS - 1), cols, chans), F32)],
            work,
            tile, *frame, dy,
        )
        grads.append(
            call(
                input_kernel,
                shape(tile.shape, BF16),
                [
                    ext_shape,
                    pltpu.VMEM((HALF, cols + 2 * OFF, chans), F32),
                    pltpu.VMEM((HALF, cols, chans), F32),
                ],
                work,
                dy, *halo(dy), cot, taps, is_north, scalars=1,
            )
        )
        own = (g_in, g_out, g_taps, g_chan, g_bin)
        sums = own if sums is None else tuple(s + o for s, o in zip(sums, own))
    g_in, g_out, g_taps, g_chan, g_bin = sums
    axes = ("lon", "lat", "dp")
    s_in, s_out, s_chan, s_bin = lax.psum((g_in, g_out, g_chan, g_bin), axes)
    s_taps = lax.psum(g_taps, axes)
    cells_all = lax.axis_size("dp") * batch * lax.axis_size("lat") * rows * lax.axis_size("lon") * cols
    scale = 1.0 / math.sqrt(cells_all)
    in_share = chans // lax.axis_size("dp")
    out_share = hidden // lax.axis_size("dp")
    position = lax.axis_index("dp")
    s_in = lax.dynamic_slice_in_dim(s_in, position * in_share, in_share, 0)
    s_out = lax.dynamic_slice_in_dim(s_out, position * out_share, out_share, 0)
    return (
        jnp.stack(grads),
        s_in * scale,
        s_out * scale,
        s_taps.reshape(KS, KS, chans) * scale,
        s_chan[2] * scale,
        s_chan[0] * scale,
        s_chan[1] * scale,
        s_bin[0] * scale,
    )


def solution(mesh):
    field = P(("groups", "dp"), "lat", "lon", None)
    placed = (field, field, P(), P(), P(), P(), P(), P(), P(), P("lat", "lon"))
    return jax.shard_map(
        local,
        mesh=mesh,
        in_specs=placed,
        out_specs=(
            field,
            P(("groups", "dp"), None),
            P(("groups", "dp"), None),
            P("groups", None, None),
            P("groups"),
            P("groups"),
            P("groups"),
            P("groups"),
        ),
        check_vma=False,
    )
```

time: 611 us -> 363 us (0.59)
  matrix products: 218 us -> 0 us
  Pallas kernels: 0 us -> 157 us
  other arithmetic: 110 us -> 4.97 us
  local copies, waits for them, and re-layouts: 66.8 us -> 11.4 us
  waiting for transfers between devices: 115 us -> 94.8 us
    conv_general_dilated x4 -> x0, matrix products: 159 us -> none  [the longest x1 90.3 us: kernel_grad(): lax.conv_general_dilated(extended[None], delta[:, :, None, :], (1, 1), 'V...]
    pallas_call x0 -> x3, Pallas kernels: none -> 157 us  [call(): pl.pallas_call(kernel, out_shape=out_shape, in_specs=[vmem] * (len(args)...]
    dot_general x20 -> x0, matrix products: 58.9 us -> none  [the longest x4 15.7 us: cell_grads(): lax.dot_general(outgrad, w_out, (((1,), (1,)), ((), ())), preferred_eleme...]
    concatenate x3 -> x4, other arithmetic: 50.3 us -> 0.23 us  [the longest x2 0.11 us: halo(): jnp.concatenate([south[:, cols - HALF:], tile[:, cols - HALF:], north[:,...]
    reduce_sum x9 -> x0, other arithmetic: 23.9 us -> none  [the longest x4 10.6 us: cell_grads(): rstd = lax.rsqrt(jnp.mean(center * center, -1, keepdims=True) + EPS)]
    unnamed x52 -> x22, local copies, waits for them, and re-layouts: 25.1 us -> 3.81 us
    ppermute x12 -> x10, waiting for transfers between devices: 24.2 us -> 7.47 us  [the longest x2 5.39 us: halo(): above = lax.ppermute(tile[:HALF], 'lat', down)]
    dynamic_update_slice x4 -> x0, other arithmetic: 16.5 us -> none  [local(): lax.scan(step, totals, (to_blocks(field_y), to_blocks(cotangent), masks))]
  transfers between devices with their start and end apart: 13 -> 11, of which waited for: 5 -> 4; matrix products, arithmetic and copies ran while one was open for 17% -> 3% of each run, Pallas kernels for 0% -> 13%
where the time goes in v1:
time: 363 us; the launch traced here: 362 us
  Pallas kernels  157 us (43%)
  waiting for transfers between devices  94.8 us (26%)
  blocking collectives  57.7 us (16%)
  starting transfers between devices  21.9 us (6%)
  between operations  14.3 us (4%)
  local copies, waits for them, and re-layouts  11.4 us (3%)
  other arithmetic  4.97 us (1%)
    pallas_call x3, Pallas kernels, call(): pl.pallas_call(kernel, out_shape=out_shape, in_specs=[vmem] * (len(args)...  157 us
    psum x1, waiting for transfers between devices, local(): s_in, s_out, s_chan, s_bin = lax.psum((g_in, g_out, g_chan, g_bin), axes)  87.3 us
    psum x1, blocking collectives, local(): s_taps = lax.psum(g_taps, axes)  57.7 us
  transfers between devices with their start and end apart: 11, of which 4 were waited for; matrix products, arithmetic and copies ran while one was open for 3% of the time, Pallas kernels for 13%

profile of v1, /device:TPU:0, one launch (start us, length us, event | category | flops | bytes accessed | tf_op | source)
XLA Modules:
  0.0 362.1 jit_solution(6982955040480594038)
XLA Ops:
  7.2 0.0 all-reduce.4.cloned.1.call-start
  7.2 1.1 slice_bitcast_fusion
  8.3 5.1 %collective-permute-start.1 = (bf16[3,256,128]{2,1,0:T(8,128)(2,1)S(1)}, bf16[3,256,128]{2,1,0:T(8,128)(2,1)S(1)}, u32[]{:S(2)}, u32[]{:S(2)}) collective-permute-start(bf16[3,256,128]{2,1,0:T(8,128)(2,1)S(1)} %get-tuple-element.30), channel_id=1, source_target_pairs={{0,12},{4,8},{8,4},{12,0},{1,13},{5,9},{9,5},{13,1},{2,14},{6,10},... | collective-permute-start | bytes 589832 | tf_op jit(solution)/shard_map/ppermute | solution.py:212
  13.4 3.4 collective-permute-start
  16.8 1.3 collective-permute-start.2
  18.1 1.0 fusion.2
  19.1 0.0 collective-permute-done.1
  19.1 0.2 rev.6
  19.4 5.4 %collective-permute-done.2 = bf16[3,256,128]{2,1,0:T(8,128)(2,1)S(1)} collective-permute-done((bf16[3,256,128]{2,1,0:T(8,128)(2,1)S(1)}, bf16[3,256,128]{2,1,0:T(8,128)(2,1)S(1)}, u32[]{:S(2)}, u32[]{:S(2)}) %collective-permute-start.2) | collective-permute-done | bytes 196640 | tf_op jit(solution)/shard_map/ppermute | solution.py:211
  24.8 0.0 copy-start.4
  24.8 0.1 pad_maximum_fusion
  24.9 0.1 collective-permute-start.3
  25.0 0.1 pad_maximum_fusion.1
  25.0 3.9 %collective-permute-start.4 = (bf16[70,3,128]{2,1,0:T(4,128)(2,1)S(1)}, bf16[70,3,128]{2,1,0:T(4,128)(2,1)S(1)}, u32[]{:S(2)}, u32[]{:S(2)}) collective-permute-start(bf16[70,3,128]{2,1,0:T(4,128)(2,1)S(1)} %pad_maximum_fusion.1), channel_id=1, source_target_pairs={{4,0},{8,4},{12,8},{0,12},{5,1},{9,5},{13,9},{1,13},{6,2},{10,6},{... | collective-permute-start | bytes 161288 | tf_op jit(solution)/shard_map/ppermute | solution.py:218
  28.9 0.7 convert_bitcast_fusion
  29.6 0.1 broadcast_in_dim.30
  29.6 0.1 convert_element_type.10
  29.7 0.7 reshape.39
  30.4 1.6 copy.19
  32.0 1.6 copy.18
  33.6 0.0 collective-permute-done.3.west
  33.6 0.7 broadcast_in_dim.31.mask
  34.4 0.7 broadcast_in_dim.34.taps
  35.1 71.7 %shard_map.161 = (bf16[64,256,128]{2,1,0:T(8,128)(2,1)}, f32[128,256]{1,0:T(8,128)}, f32[256,128]{1,0:T(8,128)}, f32[3,128]{1,0:T(4,128)}, f32[1,256]{1,0:T(1,128)}) custom-call(bf16[64,256,128]{2,1,0:T(8,128)(2,1)} %bitcast.24, bf16[3,256,128]{2,1,0:T(8,128)(2,1)} %copy-done.4, bf16[3,256,128]{2,1,0:T(8,128)(2,1)} %copy-done, ...), custom_call_target="tpu_custom_call" | custom-call | flops 26306674688 | bytes 12582912 | tf_op jit(solution)/shard_map/pallas_call | solution.py:225
  106.8 1.0 fusion
  107.8 1.0 fusion.1
  108.9 0.0 copy-start.3
  108.9 1.5 collective-permute-start.6
  110.4 1.4 collective-permute-start.5
  111.8 47.7 %shard_map.163 = f32[49,128]{1,0:T(8,128)} custom-call(bf16[64,256,128]{2,1,0:T(8,128)(2,1)} %bitcast.25, bf16[3,256,128]{2,1,0:T(8,128)(2,1)} %copy-done.4, bf16[3,256,128]{2,1,0:T(8,128)(2,1)} %copy-done, bf16[70,3,128]{2,1,0:T(4,128)(2,1)} %copy-done.6, bf16[70,3,128]{2,1,0:T(4,128)(2,1)} %copy-done.7, bf16[64,256,128]{2,1,0:T(8,128)(2,1)} %get-tuple-element.13.tile.dy), custom_call_target="tpu_custom_call" | custom-call | flops 26306674688 | bytes 12582912 | tf_op jit(solution)/shard_map/pallas_call | solution.py:225
  159.6 57.7 %all-reduce = (f32[49,128]{1,0:T(8,128)S(1)}, f32[3,128]{1,0:T(4,128)S(1)}, f32[1,256]{1,0:T(1,128)S(1)}) all-reduce(f32[49,128]{1,0:T(8,128)} %shard_map.163, f32[3,128]{1,0:T(4,128)S(1)} %copy-done.2, f32[1,256]{1,0:T(1,128)S(1)} %copy-done.3), channel_id=1, replica_groups=mesh['groups'=2,'lon'=4,'lat'=2,'dp'=2] {'lon','lat','dp'}, use_global_device_ids=true, to_apply=%region_2.3 | all-reduce | flops 6912 | bytes 55296 | tf_op jit(solution)/shard_map/psum | solution.py:297
  217.2 0.5 multiply_bitcast_fusion
  217.8 1.3 collective-permute-start.7
  219.0 0.0 all-reduce.4.cloned.1.call-update
  219.1 0.6 broadcast_multiply_fusion.1
  219.6 0.6 mul.62
  220.3 87.3 %all-reduce.4.cloned.1.call-done = (f32[128,256]{1,0:T(8,128)}, f32[256,128]{1,0:T(8,128)}) async-done(((f32[128,256]{1,0:T(8,128)}, f32[256,128]{1,0:T(8,128)}), (f32[128,256]{1,0:T(8,128)}, f32[256,128]{1,0:T(8,128)})) %all-reduce.4.cloned.1.call-update) | async-done | bytes 262160 | tf_op jit(solution)/shard_map/psum | solution.py:296
  307.6 1.5 dynamic-slice_multiply_fusion.1
  309.0 0.2 rev.7
  309.3 0.1 pad_maximum_fusion.2
  309.4 3.0 collective-permute-start.8
  312.4 0.1 pad_maximum_fusion.3
  312.4 1.0 collective-permute-start.9
  313.4 1.5 dynamic-slice_multiply_fusion
  314.9 1.4 collective-permute-done.8.west
  316.3 0.7 collective-permute-done.9.east
  317.0 0.6 copy-done.9
  317.6 37.7 %shard_map.162 = bf16[64,256,128]{2,1,0:T(8,128)(2,1)} custom-call(bf16[64,256,128]{2,1,0:T(8,128)(2,1)} %get-tuple-element.13.tile.dy, bf16[3,256,128]{2,1,0:T(8,128)(2,1)} %copy-done.5, bf16[3,256,128]{2,1,0:T(8,128)(2,1)} %copy-done.1, bf16[70,3,128]{2,1,0:T(4,128)(2,1)} %copy-done.8, bf16[70,3,128]{2,1,0:T(4,128)(2,1)} %copy-done.9, ...), custom_call_target="tpu_custom_call" | custom-call | flops 26306674688 | bytes 12582912 | tf_op jit(solution)/shard_map/pallas_call | solution.py:225
  (29 shorter events, 0.1 us)
Async XLA Ops:
  7.2 300.4 %all-reduce.4.cloned.1.call-start = ((), (), s32[]{:S(2)}) async-start(), calls=%async_computation | async-start | bytes 524288 | tf_op jit(solution)/shard_map/psum | solution.py:296
  8.3 10.9 %collective-permute-start.1 = (bf16[3,256,128]{2,1,0:T(8,128)(2,1)S(1)}, bf16[3,256,128]{2,1,0:T(8,128)(2,1)S(1)}, u32[]{:S(2)}, u32[]{:S(2)}) collective-permute-start(bf16[3,256,128]{2,1,0:T(8,128)(2,1)S(1)} %get-tuple-element.30), channel_id=1, source_target_pairs={{0,12},{4,8},{8,4},{12,0},{1,13},{5,9},{9,5},{13,1},{2,14},{6,10},... | collective-permute-start | bytes 589832 | tf_op jit(solution)/shard_map/ppermute | solution.py:212
  13.4 11.4 %collective-permute-start = (bf16[3,256,128]{2,1,0:T(8,128)(2,1)S(1)}, bf16[3,256,128]{2,1,0:T(8,128)(2,1)S(1)}, u32[]{:S(2)}, u32[]{:S(2)}) collective-permute-start(bf16[3,256,128]{2,1,0:T(8,128)(2,1)S(1)} %get-tuple-element.30), channel_id=1, source_target_pairs={{0,2},{1,3},{4,6},{5,7},{8,10},{9,11},{12,14},{13,15},{16,18},{17,... | collective-permute-start | bytes 589832 | tf_op jit(solution)/shard_map/ppermute | solution.py:210
  16.8 8.0 %collective-permute-start.2 = (bf16[3,256,128]{2,1,0:T(8,128)(2,1)S(1)}, bf16[3,256,128]{2,1,0:T(8,128)(2,1)S(1)}, u32[]{:S(2)}, u32[]{:S(2)}) collective-permute-start(bf16[3,256,128]{2,1,0:T(8,128)(2,1)S(1)} %get-tuple-element.29), channel_id=1, source_target_pairs={{2,0},{3,1},{6,4},{7,5},{10,8},{11,9},{14,12},{15,13},{18,16},{19,... | collective-permute-start | bytes 589832 | tf_op jit(solution)/shard_map/ppermute | solution.py:211
  24.8 10.3 %copy-start = (bf16[3,256,128]{2,1,0:T(8,128)(2,1)}, bf16[3,256,128]{2,1,0:T(8,128)(2,1)S(1)}, u32[]{:S(2)}) copy-start(bf16[3,256,128]{2,1,0:T(8,128)(2,1)S(1)} %broadcast_select_fusion.1.north) | copy-start | bytes 589828
  24.8 10.2 %copy-start.4 = (bf16[3,256,128]{2,1,0:T(8,128)(2,1)}, bf16[3,256,128]{2,1,0:T(8,128)(2,1)S(1)}, u32[]{:S(2)}) copy-start(bf16[3,256,128]{2,1,0:T(8,128)(2,1)S(1)} %collective-permute-done.south) | copy-start | bytes 589828
  24.9 8.7 %collective-permute-start.3 = (bf16[70,3,128]{2,1,0:T(4,128)(2,1)S(1)}, bf16[70,3,128]{2,1,0:T(4,128)(2,1)S(1)}, u32[]{:S(2)}, u32[]{:S(2)}) collective-permute-start(bf16[70,3,128]{2,1,0:T(4,128)(2,1)S(1)} %pad_maximum_fusion), channel_id=1, source_target_pairs={{0,4},{4,8},{8,12},{12,0},{1,5},{5,9},{9,13},{13,1},{2,6},{6,10},{... | collective-permute-start | bytes 161288 | tf_op jit(solution)/shard_map/ppermute | solution.py:217
  25.0 8.6 %collective-permute-start.4 = (bf16[70,3,128]{2,1,0:T(4,128)(2,1)S(1)}, bf16[70,3,128]{2,1,0:T(4,128)(2,1)S(1)}, u32[]{:S(2)}, u32[]{:S(2)}) collective-permute-start(bf16[70,3,128]{2,1,0:T(4,128)(2,1)S(1)} %pad_maximum_fusion.1), channel_id=1, source_target_pairs={{4,0},{8,4},{12,8},{0,12},{5,1},{9,5},{13,9},{1,13},{6,2},{10,6},{... | collective-permute-start | bytes 161288 | tf_op jit(solution)/shard_map/ppermute | solution.py:218
  33.6 1.5 copy-start.6
  33.6 1.4 copy-start.7
  108.9 50.7 %copy-start.2 = (f32[3,128]{1,0:T(4,128)S(1)}, f32[3,128]{1,0:T(4,128)}, u32[]{:S(2)}) copy-start(f32[3,128]{1,0:T(4,128)} %get-tuple-element.16) | copy-start | bytes 4612
  108.9 50.7 %copy-start.3 = (f32[1,256]{1,0:T(1,128)S(1)}, f32[1,256]{1,0:T(1,128)}, u32[]{:S(2)}) copy-start(f32[1,256]{1,0:T(1,128)} %get-tuple-element.17) | copy-start | bytes 3076
  108.9 200.1 %collective-permute-start.6 = (bf16[3,256,128]{2,1,0:T(8,128)(2,1)S(1)}, bf16[3,256,128]{2,1,0:T(8,128)(2,1)S(1)}, u32[]{:S(2)}, u32[]{:S(2)}) collective-permute-start(bf16[3,256,128]{2,1,0:T(8,128)(2,1)S(1)} %get-tuple-element.26), channel_id=1, source_target_pairs={{0,12},{4,8},{8,4},{12,0},{1,13},{5,9},{9,5},{13,1},{2,14},{6,10},... | collective-permute-start | bytes 589832 | tf_op jit(solution)/shard_map/ppermute | solution.py:212
  110.4 198.9 %collective-permute-start.5 = (bf16[3,256,128]{2,1,0:T(8,128)(2,1)S(1)}, bf16[3,256,128]{2,1,0:T(8,128)(2,1)S(1)}, u32[]{:S(2)}, u32[]{:S(2)}) collective-permute-start(bf16[3,256,128]{2,1,0:T(8,128)(2,1)S(1)} %get-tuple-element.26), channel_id=1, source_target_pairs={{0,2},{1,3},{4,6},{5,7},{8,10},{9,11},{12,14},{13,15},{16,18},{17,... | collective-permute-start | bytes 589832 | tf_op jit(solution)/shard_map/ppermute | solution.py:210
  217.8 91.5 %collective-permute-start.7 = (bf16[3,256,128]{2,1,0:T(8,128)(2,1)S(1)}, bf16[3,256,128]{2,1,0:T(8,128)(2,1)S(1)}, u32[]{:S(2)}, u32[]{:S(2)}) collective-permute-start(bf16[3,256,128]{2,1,0:T(8,128)(2,1)S(1)} %get-tuple-element.25), channel_id=1, source_target_pairs={{2,0},{3,1},{6,4},{7,5},{10,8},{11,9},{14,12},{15,13},{18,16},{19,... | collective-permute-start | bytes 589832 | tf_op jit(solution)/shard_map/ppermute | solution.py:211
  309.3 7.7 %copy-start.1 = (bf16[3,256,128]{2,1,0:T(8,128)(2,1)}, bf16[3,256,128]{2,1,0:T(8,128)(2,1)S(1)}, u32[]{:S(2)}) copy-start(bf16[3,256,128]{2,1,0:T(8,128)(2,1)S(1)} %broadcast_select_fusion.north) | copy-start | bytes 589828
  309.3 7.6 %copy-start.5 = (bf16[3,256,128]{2,1,0:T(8,128)(2,1)}, bf16[3,256,128]{2,1,0:T(8,128)(2,1)S(1)}, u32[]{:S(2)}) copy-start(bf16[3,256,128]{2,1,0:T(8,128)(2,1)S(1)} %collective-permute-done.5.south) | copy-start | bytes 589828
  309.4 6.9 %collective-permute-start.8 = (bf16[70,3,128]{2,1,0:T(4,128)(2,1)S(1)}, bf16[70,3,128]{2,1,0:T(4,128)(2,1)S(1)}, u32[]{:S(2)}, u32[]{:S(2)}) collective-permute-start(bf16[70,3,128]{2,1,0:T(4,128)(2,1)S(1)} %pad_maximum_fusion.2), channel_id=1, source_target_pairs={{0,4},{4,8},{8,12},{12,0},{1,5},{5,9},{9,13},{13,1},{2,6},{6,10},{... | collective-permute-start | bytes 161288 | tf_op jit(solution)/shard_map/ppermute | solution.py:217
  312.4 4.5 %collective-permute-start.9 = (bf16[70,3,128]{2,1,0:T(4,128)(2,1)S(1)}, bf16[70,3,128]{2,1,0:T(4,128)(2,1)S(1)}, u32[]{:S(2)}, u32[]{:S(2)}) collective-permute-start(bf16[70,3,128]{2,1,0:T(4,128)(2,1)S(1)} %pad_maximum_fusion.3), channel_id=1, source_target_pairs={{4,0},{8,4},{12,8},{0,12},{5,1},{9,5},{13,9},{1,13},{6,2},{10,6},{... | collective-permute-start | bytes 161288 | tf_op jit(solution)/shard_map/ppermute | solution.py:218
  316.3 0.7 copy-start.8
  316.9 0.6 copy-start.9
Sparse Core Ops, SparseCore 0:
  219.2 88.3 all-reduce.3

commit v2 on v1

--- a/solution.py
+++ b/solution.py
@@ -149,8 +149,8 @@
         def row_step(rho, acc):
             def col_step(j, acc):
                 acc = list(acc)
-                for sub in range(4):
-                    c0 = pl.multiple_of(j * 32 + sub * 8, 8)
+                for sub in range(8):
+                    c0 = pl.multiple_of(j * 64 + sub * 8, 8)
                     d = [dyf[rho + (KS - 1) - a, pl.ds(c0, 8), :] for a in range(first, last)]
                     for b in range(KS):
                         v = ext[rho, pl.ds(c0 + (OFF - HALF + b), 8), :]
@@ -159,7 +159,7 @@
                             acc[at] = acc[at] + v * d[q]
                 return tuple(acc)
 
-            return lax.fori_loop(0, cols // 32, col_step, acc)
+            return lax.fori_loop(0, cols // 64, col_step, acc)
 
         zero = jnp.zeros((8, chans), F32)
         acc = lax.fori_loop(0, rows + KS - 1, row_step, (zero,) * (KS * (last - first)))
@@ -231,6 +231,26 @@
         compiler_params=pltpu.CompilerParams(vmem_limit_bytes=56 * 1024 * 1024),
         cost_estimate=pl.CostEstimate(flops=flops, bytes_accessed=12 << 20, transcendentals=0),
     )(*args)
+
+
+def axis_sum(x, axis):
+    count = lax.axis_size(axis)
+    if count & (count - 1):
+        return lax.psum(x, axis)
+    step = 1
+    while step < count:
+        x = x + lax.ppermute(x, axis, [(i, i ^ step) for i in range(count)])
+        step *= 2
+    return x
+
+
+def dp_share(x, share):
+    count, at = lax.axis_size("dp"), lax.axis_index("dp")
+    if count != 2:
+        return lax.dynamic_slice_in_dim(lax.psum(x, "dp"), at * share, share, 0)
+    mine = lax.dynamic_slice_in_dim(x, at * share, share, 0)
+    theirs = lax.dynamic_slice_in_dim(x, (1 - at) * share, share, 0)
+    return mine + lax.ppermute(theirs, "dp", [(0, 1), (1, 0)])
 
 
 def local(inputs, cotangent, kernel_dw, bias_dw, gain, shift_ln, w_in, b_in, w_out, ocean_mask):
@@ -292,16 +312,23 @@
         own = (g_in, g_out, g_taps, g_chan, g_bin)
         sums = own if sums is None else tuple(s + o for s, o in zip(sums, own))
     g_in, g_out, g_taps, g_chan, g_bin = sums
-    axes = ("lon", "lat", "dp")
-    s_in, s_out, s_chan, s_bin = lax.psum((g_in, g_out, g_chan, g_bin), axes)
-    s_taps = lax.psum(g_taps, axes)
     cells_all = lax.axis_size("dp") * batch * lax.axis_size("lat") * rows * lax.axis_size("lon") * cols
     scale = 1.0 / math.sqrt(cells_all)
     in_share = chans // lax.axis_size("dp")
     out_share = hidden // lax.axis_size("dp")
-    position = lax.axis_index("dp")
-    s_in = lax.dynamic_slice_in_dim(s_in, position * in_share, in_share, 0)
-    s_out = lax.dynamic_slice_in_dim(s_out, position * out_share, out_share, 0)
+    halves = (
+        dp_share(g_in, in_share).reshape(-1, chans),
+        dp_share(g_out, out_share),
+        axis_sum(jnp.concatenate([g_chan, g_bin.reshape(-1, chans)], 0), "dp"),
+    )
+    total = jnp.concatenate([*halves, g_taps], 0)
+    for axis in ("lat", "lon"):
+        total = axis_sum(total, axis)
+    in_rows = in_share * hidden // chans
+    parts = jnp.split(total, (in_rows, in_rows + out_share, in_rows + out_share + 3, total.shape[0] - KS * KS))
+    s_in, s_out, s_chan, s_bin, s_taps = parts
+    s_in, s_bin = s_in.reshape(in_share, hidden), s_bin.reshape(1, hidden)
+    s_taps = axis_sum(s_taps, "dp")
     return (
         jnp.stack(grads),
         s_in * scale,

time: 363 us -> 214 us (0.59)
  waiting for transfers between devices: 94.8 us -> 16.8 us
  blocking collectives: 57.7 us -> 0 us
  between operations: 14.3 us -> 1.03 us
  Pallas kernels: 157 us -> 151 us
    psum x1 -> x0, waiting for transfers between devices: 87.3 us -> none  [local(): s_in, s_out, s_chan, s_bin = lax.psum((g_in, g_out, g_chan, g_bin), axes)]
    psum x1 -> x0, blocking collectives: 57.7 us -> none  [local(): s_taps = lax.psum(g_taps, axes)]
    ppermute x0 -> x7, waiting for transfers between devices: none -> 6.94 us  [the longest x5 6.94 us: axis_sum(): x = x + lax.ppermute(x, axis, [(i, i ^ step) for i in range(count)])]
    pallas_call x3, Pallas kernels: 157 us -> 151 us  [call(): pl.pallas_call(kernel, out_shape=out_shape, in_specs=[vmem] * (len(args)...]
    ppermute x0 -> x7, starting transfers between devices: none -> 4.48 us  [the longest x5 3.91 us: axis_sum(): x = x + lax.ppermute(x, axis, [(i, i ^ step) for i in range(count)])]
    ppermute x2, waiting for transfers between devices: 5.39 us -> 9.85 us  [halo(): above = lax.ppermute(tile[:HALF], 'lat', down)]
  transfers between devices with their start and end apart: 11 -> 17, of which waited for: 4 -> 4; matrix products, arithmetic and copies ran while one was open for 3% -> 5% of each run, Pallas kernels for 13% -> 37%
where the time goes in v2:
time: 214 us; the launch traced here: 213 us
  Pallas kernels  151 us (71%)
  starting transfers between devices  24.9 us (12%)
  waiting for transfers between devices  16.8 us (8%)
  local copies, waits for them, and re-layouts  13.8 us (6%)
  other arithmetic  4.98 us (2%)
    pallas_call x3, Pallas kernels, call(): pl.pallas_call(kernel, out_shape=out_shape, in_specs=[vmem] * (len(args)...  151 us
    ppermute x2, waiting for transfers between devices, halo(): above = lax.ppermute(tile[:HALF], 'lat', down)  9.85 us
    ppermute x5, waiting for transfers between devices, axis_sum(): x = x + lax.ppermute(x, axis, [(i, i ^ step) for i in range(count)])  6.94 us
    ppermute x2, starting transfers between devices, halo(): lax.ppermute(tile[rows - HALF:], 'lon', [(i, lons - 1 - i) for i in range...  6.59 us
    ppermute x2, starting transfers between devices, halo(): east = lax.ppermute(left, 'lon', [((i + 1) % lons, i) for i in range(lons)])  6.32 us
    ppermute x2, starting transfers between devices, halo(): south = lax.ppermute(tile[rows - HALF:], 'lat', up)  4.85 us
  transfers between devices with their start and end apart: 17, of which 4 were waited for; matrix products, arithmetic and copies ran while one was open for 5% of the time, Pallas kernels for 37%

profile of v2, /device:TPU:0, one launch (start us, length us, event | category | flops | bytes accessed | tf_op | source)
XLA Modules:
  0.0 213.0 jit_solution(4286625176787921230)
XLA Ops:
  0.6 1.1 slice_bitcast_fusion
  1.7 5.1 %collective-permute-start.1 = (bf16[3,256,128]{2,1,0:T(8,128)(2,1)S(1)}, bf16[3,256,128]{2,1,0:T(8,128)(2,1)S(1)}, u32[]{:S(2)}, u32[]{:S(2)}) collective-permute-start(bf16[3,256,128]{2,1,0:T(8,128)(2,1)S(1)} %get-tuple-element.25), channel_id=1, source_target_pairs={{0,12},{4,8},{8,4},{12,0},{1,13},{5,9},{9,5},{13,1},{2,14},{6,10},... | collective-permute-start | bytes 589832 | tf_op jit(solution)/shard_map/ppermute | solution.py:212
  6.8 3.4 %collective-permute-start = (bf16[3,256,128]{2,1,0:T(8,128)(2,1)S(1)}, bf16[3,256,128]{2,1,0:T(8,128)(2,1)S(1)}, u32[]{:S(2)}, u32[]{:S(2)}) collective-permute-start(bf16[3,256,128]{2,1,0:T(8,128)(2,1)S(1)} %get-tuple-element.25), channel_id=1, source_target_pairs={{0,2},{1,3},{4,6},{5,7},{8,10},{9,11},{12,14},{13,15},{16,18},{17,... | collective-permute-start | bytes 589832 | tf_op jit(solution)/shard_map/ppermute | solution.py:210
  10.2 1.3 collective-permute-start.2
  11.5 1.0 fusion.7
  12.5 0.2 rev.6
  12.8 5.4 %collective-permute-done.2 = bf16[3,256,128]{2,1,0:T(8,128)(2,1)S(1)} collective-permute-done((bf16[3,256,128]{2,1,0:T(8,128)(2,1)S(1)}, bf16[3,256,128]{2,1,0:T(8,128)(2,1)S(1)}, u32[]{:S(2)}, u32[]{:S(2)}) %collective-permute-start.2) | collective-permute-done | bytes 196640 | tf_op jit(solution)/shard_map/ppermute | solution.py:211
  18.3 0.1 pad_maximum_fusion.1
  18.3 0.1 collective-permute-start.3
  18.5 3.9 %collective-permute-start.4 = (bf16[70,3,128]{2,1,0:T(4,128)(2,1)S(1)}, bf16[70,3,128]{2,1,0:T(4,128)(2,1)S(1)}, u32[]{:S(2)}, u32[]{:S(2)}) collective-permute-start(bf16[70,3,128]{2,1,0:T(4,128)(2,1)S(1)} %pad_maximum_fusion.2), channel_id=1, source_target_pairs={{4,0},{8,4},{12,8},{0,12},{5,1},{9,5},{13,9},{1,13},{6,2},{10,6},{... | collective-permute-start | bytes 161288 | tf_op jit(solution)/shard_map/ppermute | solution.py:218
  22.3 0.7 convert_bitcast_fusion
  23.0 0.1 broadcast_in_dim.30
  23.1 0.1 convert_element_type.10
  23.1 0.7 reshape.50
  23.9 1.6 copy.19
  25.4 1.6 copy.18
  27.0 0.7 broadcast_in_dim.31.mask
  27.8 0.7 broadcast_in_dim.34.taps
  28.5 71.8 %shard_map.161 = (bf16[64,256,128]{2,1,0:T(8,128)(2,1)}, f32[128,256]{1,0:T(8,128)}, f32[256,128]{1,0:T(8,128)}, f32[3,128]{1,0:T(4,128)}, f32[1,256]{1,0:T(1,128)}) custom-call(bf16[64,256,128]{2,1,0:T(8,128)(2,1)} %bitcast.26, bf16[3,256,128]{2,1,0:T(8,128)(2,1)} %copy-done.6, bf16[3,256,128]{2,1,0:T(8,128)(2,1)} %copy-done, ...), custom_call_target="tpu_custom_call" | custom-call | flops 26306674688 | bytes 12582912 | tf_op jit(solution)/shard_map/pallas_call | solution.py:225
  100.3 1.0 fusion.5
  101.3 1.0 fusion.6
  102.3 1.5 collective-permute-start.6
  103.8 1.5 collective-permute-start.5
  105.3 0.7 pad_maximum_fusion.5
  106.0 0.9 constant_dynamic-slice_fusion
  106.8 0.5 collective-permute-start.11
  107.3 0.8 constant_dynamic-slice_fusion.1
  108.2 0.1 collective-permute-start.10
  108.3 42.0 %shard_map.163 = f32[49,128]{1,0:T(8,128)} custom-call(bf16[64,256,128]{2,1,0:T(8,128)(2,1)} %bitcast.27, bf16[3,256,128]{2,1,0:T(8,128)(2,1)} %copy-done.6, bf16[3,256,128]{2,1,0:T(8,128)(2,1)} %copy-done, bf16[70,3,128]{2,1,0:T(4,128)(2,1)} %copy-done.8, bf16[70,3,128]{2,1,0:T(4,128)(2,1)} %copy-done.9, bf16[64,256,128]{2,1,0:T(8,128)(2,1)} %get-tuple-element.13.tile.dy), custom_call_target="tpu_custom_call" | custom-call | flops 26306674688 | bytes 12582912 | tf_op jit(solution)/shard_map/pallas_call | solution.py:225
  150.3 1.3 collective-permute-start.7
  151.7 0.8 pad_maximum_fusion
  152.5 2.7 %collective-permute-start.13 = (f32[310,128]{1,0:T(8,128)S(1)}, f32[310,128]{1,0:T(8,128)S(1)}, u32[]{:S(2)}, u32[]{:S(2)}) collective-permute-start(f32[310,128]{1,0:T(8,128)S(1)} %pad_maximum_fusion), channel_id=1, source_target_pairs={{0,2},{2,0},{1,3},{3,1},{4,6},{6,4},{5,7},{7,5},{8,10},{10,8},{9,1... | collective-permute-start | bytes 476168 | tf_op jit(solution)/shard_map/ppermute | solution.py:242
  155.2 0.2 rev.7
  155.4 4.5 %collective-permute-done.7 = bf16[3,256,128]{2,1,0:T(8,128)(2,1)S(1)} collective-permute-done((bf16[3,256,128]{2,1,0:T(8,128)(2,1)S(1)}, bf16[3,256,128]{2,1,0:T(8,128)(2,1)S(1)}, u32[]{:S(2)}, u32[]{:S(2)}) %collective-permute-start.7) | collective-permute-done | bytes 196640 | tf_op jit(solution)/shard_map/ppermute | solution.py:211
  160.0 0.1 collective-permute-start.8
  160.1 2.8 %collective-permute-done.13 = f32[310,128]{1,0:T(8,128)S(1)} collective-permute-done((f32[310,128]{1,0:T(8,128)S(1)}, f32[310,128]{1,0:T(8,128)S(1)}, u32[]{:S(2)}, u32[]{:S(2)}) %collective-permute-start.13) | collective-permute-done | bytes 158752 | tf_op jit(solution)/shard_map/ppermute | solution.py:242
  162.9 0.8 fusion.12
  163.7 0.1 collective-permute-start.14
  163.8 2.5 %collective-permute-start.9 = (bf16[70,3,128]{2,1,0:T(4,128)(2,1)S(1)}, bf16[70,3,128]{2,1,0:T(4,128)(2,1)S(1)}, u32[]{:S(2)}, u32[]{:S(2)}) collective-permute-start(bf16[70,3,128]{2,1,0:T(4,128)(2,1)S(1)} %pad_maximum_fusion.4), channel_id=1, source_target_pairs={{4,0},{8,4},{12,8},{0,12},{5,1},{9,5},{13,9},{1,13},{6,2},{10,6},{... | collective-permute-start | bytes 161288 | tf_op jit(solution)/shard_map/ppermute | solution.py:218
  166.3 4.2 %collective-permute-done.14 = f32[310,128]{1,0:T(8,128)S(1)} collective-permute-done((f32[310,128]{1,0:T(8,128)S(1)}, f32[310,128]{1,0:T(8,128)S(1)}, u32[]{:S(2)}, u32[]{:S(2)}) %collective-permute-start.14) | collective-permute-done | bytes 158752 | tf_op jit(solution)/shard_map/ppermute | solution.py:242
  170.4 1.1 collective-permute-start.15
  171.6 0.6 copy-done.10
  172.2 37.7 %shard_map.162 = bf16[64,256,128]{2,1,0:T(8,128)(2,1)} custom-call(bf16[64,256,128]{2,1,0:T(8,128)(2,1)} %get-tuple-element.13.tile.dy, bf16[3,256,128]{2,1,0:T(8,128)(2,1)} %copy-done.7, bf16[3,256,128]{2,1,0:T(8,128)(2,1)} %copy-done.1, bf16[70,3,128]{2,1,0:T(4,128)(2,1)} %copy-done.10, bf16[70,3,128]{2,1,0:T(4,128)(2,1)} %copy-done.11, ...), custom_call_target="tpu_custom_call" | custom-call | flops 26306674688 | bytes 12582912 | tf_op jit(solution)/shard_map/pallas_call | solution.py:225
  210.0 0.5 fusion.1
  210.5 0.6 slice_multiply_fusion
  211.2 0.6 fusion
  211.7 0.6 mul.67
  212.4 0.6 mul.71
  (55 shorter events, 0.5 us)
Async XLA Ops:
  1.7 10.9 %collective-permute-start.1 = (bf16[3,256,128]{2,1,0:T(8,128)(2,1)S(1)}, bf16[3,256,128]{2,1,0:T(8,128)(2,1)S(1)}, u32[]{:S(2)}, u32[]{:S(2)}) collective-permute-start(bf16[3,256,128]{2,1,0:T(8,128)(2,1)S(1)} %get-tuple-element.25), channel_id=1, source_target_pairs={{0,12},{4,8},{8,4},{12,0},{1,13},{5,9},{9,5},{13,1},{2,14},{6,10},... | collective-permute-start | bytes 589832 | tf_op jit(solution)/shard_map/ppermute | solution.py:212
  6.8 11.4 %collective-permute-start = (bf16[3,256,128]{2,1,0:T(8,128)(2,1)S(1)}, bf16[3,256,128]{2,1,0:T(8,128)(2,1)S(1)}, u32[]{:S(2)}, u32[]{:S(2)}) collective-permute-start(bf16[3,256,128]{2,1,0:T(8,128)(2,1)S(1)} %get-tuple-element.25), channel_id=1, source_target_pairs={{0,2},{1,3},{4,6},{5,7},{8,10},{9,11},{12,14},{13,15},{16,18},{17,... | collective-permute-start | bytes 589832 | tf_op jit(solution)/shard_map/ppermute | solution.py:210
  10.2 8.0 %collective-permute-start.2 = (bf16[3,256,128]{2,1,0:T(8,128)(2,1)S(1)}, bf16[3,256,128]{2,1,0:T(8,128)(2,1)S(1)}, u32[]{:S(2)}, u32[]{:S(2)}) collective-permute-start(bf16[3,256,128]{2,1,0:T(8,128)(2,1)S(1)} %get-tuple-element.24), channel_id=1, source_target_pairs={{2,0},{3,1},{6,4},{7,5},{10,8},{11,9},{14,12},{15,13},{18,16},{19,... | collective-permute-start | bytes 589832 | tf_op jit(solution)/shard_map/ppermute | solution.py:211
  18.2 10.3 %copy-start = (bf16[3,256,128]{2,1,0:T(8,128)(2,1)}, bf16[3,256,128]{2,1,0:T(8,128)(2,1)S(1)}, u32[]{:S(2)}) copy-start(bf16[3,256,128]{2,1,0:T(8,128)(2,1)S(1)} %broadcast_select_fusion.1.north) | copy-start | bytes 589828
  18.2 10.3 %copy-start.6 = (bf16[3,256,128]{2,1,0:T(8,128)(2,1)}, bf16[3,256,128]{2,1,0:T(8,128)(2,1)S(1)}, u32[]{:S(2)}) copy-start(bf16[3,256,128]{2,1,0:T(8,128)(2,1)S(1)} %collective-permute-done.south) | copy-start | bytes 589828
  18.3 8.7 %collective-permute-start.3 = (bf16[70,3,128]{2,1,0:T(4,128)(2,1)S(1)}, bf16[70,3,128]{2,1,0:T(4,128)(2,1)S(1)}, u32[]{:S(2)}, u32[]{:S(2)}) collective-permute-start(bf16[70,3,128]{2,1,0:T(4,128)(2,1)S(1)} %pad_maximum_fusion.1), channel_id=1, source_target_pairs={{0,4},{4,8},{8,12},{12,0},{1,5},{5,9},{9,13},{13,1},{2,6},{6,10},{... | collective-permute-start | bytes 161288 | tf_op jit(solution)/shard_map/ppermute | solution.py:217
  18.5 8.6 %collective-permute-start.4 = (bf16[70,3,128]{2,1,0:T(4,128)(2,1)S(1)}, bf16[70,3,128]{2,1,0:T(4,128)(2,1)S(1)}, u32[]{:S(2)}, u32[]{:S(2)}) collective-permute-start(bf16[70,3,128]{2,1,0:T(4,128)(2,1)S(1)} %pad_maximum_fusion.2), channel_id=1, source_target_pairs={{4,0},{8,4},{12,8},{0,12},{5,1},{9,5},{13,9},{1,13},{6,2},{10,6},{... | collective-permute-start | bytes 161288 | tf_op jit(solution)/shard_map/ppermute | solution.py:218
  27.0 1.5 copy-start.8
  27.0 1.5 copy-start.9
  102.3 52.9 %collective-permute-start.6 = (bf16[3,256,128]{2,1,0:T(8,128)(2,1)S(1)}, bf16[3,256,128]{2,1,0:T(8,128)(2,1)S(1)}, u32[]{:S(2)}, u32[]{:S(2)}) collective-permute-start(bf16[3,256,128]{2,1,0:T(8,128)(2,1)S(1)} %get-tuple-element.21), channel_id=1, source_target_pairs={{0,12},{4,8},{8,4},{12,0},{1,13},{5,9},{9,5},{13,1},{2,14},{6,10},... | collective-permute-start | bytes 589832 | tf_op jit(solution)/shard_map/ppermute | solution.py:212
  103.8 56.1 %collective-permute-start.5 = (bf16[3,256,128]{2,1,0:T(8,128)(2,1)S(1)}, bf16[3,256,128]{2,1,0:T(8,128)(2,1)S(1)}, u32[]{:S(2)}, u32[]{:S(2)}) collective-permute-start(bf16[3,256,128]{2,1,0:T(8,128)(2,1)S(1)} %get-tuple-element.21), channel_id=1, source_target_pairs={{0,2},{1,3},{4,6},{5,7},{8,10},{9,11},{12,14},{13,15},{16,18},{17,... | collective-permute-start | bytes 589832 | tf_op jit(solution)/shard_map/ppermute | solution.py:210
  106.0 44.3 %collective-permute-start.12 = (f32[5,128]{1,0:T(8,128)S(1)}, f32[5,128]{1,0:T(8,128)S(1)}, u32[]{:S(2)}, u32[]{:S(2)}) collective-permute-start(f32[5,128]{1,0:T(8,128)S(1)} %pad_maximum_fusion.5), channel_id=1, source_target_pairs={{0,1},{1,0},{2,3},{3,2},{4,5},{5,4},{6,7},{7,6},{8,9},{9,8},{10,11... | collective-permute-start | bytes 7688 | tf_op jit(solution)/shard_map/ppermute | solution.py:242
  106.8 44.8 %collective-permute-start.11 = (f32[128,128]{1,0:T(8,128)S(1)}, f32[128,128]{1,0:T(8,128)S(1)}, u32[]{:S(2)}, u32[]{:S(2)}) collective-permute-start(f32[128,128]{1,0:T(8,128)S(1)} %constant_dynamic-slice_fusion), channel_id=1, source_target_pairs={{0,1},{1,0},{2,3},{3,2},{4,5},{5,4},{6,7},{7,6},{8,9},{9,8},{10,11... | collective-permute-start | bytes 196616 | tf_op jit(solution)/shard_map/ppermute | solution.py:253
  108.2 43.4 %copy-start.4 = (f32[3,128]{1,0:T(4,128)S(1)}, f32[3,128]{1,0:T(4,128)}, u32[]{:S(2)}) copy-start(f32[3,128]{1,0:T(4,128)} %get-tuple-element.16) | copy-start | bytes 4612
  108.2 43.4 %copy-start.5 = (f32[1,256]{1,0:T(1,128)S(1)}, f32[1,256]{1,0:T(1,128)}, u32[]{:S(2)}) copy-start(f32[1,256]{1,0:T(1,128)} %get-tuple-element.17) | copy-start | bytes 3076
  108.2 43.5 %copy-start.3 = (f32[256,128]{1,0:T(8,128)S(1)}, f32[256,128]{1,0:T(8,128)}, u32[]{:S(2)}) copy-start(f32[256,128]{1,0:T(8,128)} %get-tuple-element.15) | copy-start | bytes 393220
  108.2 43.5 %copy-start.2 = (f32[128,256]{1,0:T(8,128)S(1)}, f32[128,256]{1,0:T(8,128)}, u32[]{:S(2)}) copy-start(f32[128,256]{1,0:T(8,128)} %get-tuple-element.14) | copy-start | bytes 393220
  108.2 43.5 %collective-permute-start.10 = (f32[64,256]{1,0:T(8,128)S(1)}, f32[64,256]{1,0:T(8,128)S(1)}, u32[]{:S(2)}, u32[]{:S(2)}) collective-permute-start(f32[64,256]{1,0:T(8,128)S(1)} %constant_dynamic-slice_fusion.1), channel_id=1, source_target_pairs={{0,1},{1,0},{2,3},{3,2},{4,5},{5,4},{6,7},{7,6},{8,9},{9,8},{10,11... | collective-permute-start | bytes 196616 | tf_op jit(solution)/shard_map/ppermute | solution.py:253
  150.3 9.6 %collective-permute-start.7 = (bf16[3,256,128]{2,1,0:T(8,128)(2,1)S(1)}, bf16[3,256,128]{2,1,0:T(8,128)(2,1)S(1)}, u32[]{:S(2)}, u32[]{:S(2)}) collective-permute-start(bf16[3,256,128]{2,1,0:T(8,128)(2,1)S(1)} %get-tuple-element.20), channel_id=1, source_target_pairs={{2,0},{3,1},{6,4},{7,5},{10,8},{11,9},{14,12},{15,13},{18,16},{19,... | collective-permute-start | bytes 589832 | tf_op jit(solution)/shard_map/ppermute | solution.py:211
  152.5 10.4 %collective-permute-start.13 = (f32[310,128]{1,0:T(8,128)S(1)}, f32[310,128]{1,0:T(8,128)S(1)}, u32[]{:S(2)}, u32[]{:S(2)}) collective-permute-start(f32[310,128]{1,0:T(8,128)S(1)} %pad_maximum_fusion), channel_id=1, source_target_pairs={{0,2},{2,0},{1,3},{3,1},{4,6},{6,4},{5,7},{7,5},{8,10},{10,8},{9,1... | collective-permute-start | bytes 476168 | tf_op jit(solution)/shard_map/ppermute | solution.py:242
  159.9 11.7 %copy-start.1 = (bf16[3,256,128]{2,1,0:T(8,128)(2,1)}, bf16[3,256,128]{2,1,0:T(8,128)(2,1)S(1)}, u32[]{:S(2)}) copy-start(bf16[3,256,128]{2,1,0:T(8,128)(2,1)S(1)} %broadcast_select_fusion.north) | copy-start | bytes 589828
  160.0 11.6 %copy-start.7 = (bf16[3,256,128]{2,1,0:T(8,128)(2,1)}, bf16[3,256,128]{2,1,0:T(8,128)(2,1)S(1)}, u32[]{:S(2)}) copy-start(bf16[3,256,128]{2,1,0:T(8,128)(2,1)S(1)} %collective-permute-done.5.south) | copy-start | bytes 589828
  160.0 11.5 %collective-permute-start.8 = (bf16[70,3,128]{2,1,0:T(4,128)(2,1)S(1)}, bf16[70,3,128]{2,1,0:T(4,128)(2,1)S(1)}, u32[]{:S(2)}, u32[]{:S(2)}) collective-permute-start(bf16[70,3,128]{2,1,0:T(4,128)(2,1)S(1)} %pad_maximum_fusion.3), channel_id=1, source_target_pairs={{0,4},{4,8},{8,12},{12,0},{1,5},{5,9},{9,13},{13,1},{2,6},{6,10},{... | collective-permute-start | bytes 161288 | tf_op jit(solution)/shard_map/ppermute | solution.py:217
  163.7 6.8 %collective-permute-start.14 = (f32[310,128]{1,0:T(8,128)S(1)}, f32[310,128]{1,0:T(8,128)S(1)}, u32[]{:S(2)}, u32[]{:S(2)}) collective-permute-start(f32[310,128]{1,0:T(8,128)S(1)} %fusion.12), channel_id=1, source_target_pairs={{0,4},{4,0},{8,12},{12,8},{1,5},{5,1},{9,13},{13,9},{2,6},{6,2},{1... | collective-permute-start | bytes 476168 | tf_op jit(solution)/shard_map/ppermute | solution.py:242
  163.8 7.8 %collective-permute-start.9 = (bf16[70,3,128]{2,1,0:T(4,128)(2,1)S(1)}, bf16[70,3,128]{2,1,0:T(4,128)(2,1)S(1)}, u32[]{:S(2)}, u32[]{:S(2)}) collective-permute-start(bf16[70,3,128]{2,1,0:T(4,128)(2,1)S(1)} %pad_maximum_fusion.4), channel_id=1, source_target_pairs={{4,0},{8,4},{12,8},{0,12},{5,1},{9,5},{13,9},{1,13},{6,2},{10,6},{... | collective-permute-start | bytes 161288 | tf_op jit(solution)/shard_map/ppermute | solution.py:218
  170.4 39.5 %collective-permute-start.15 = (f32[310,128]{1,0:T(8,128)S(1)}, f32[310,128]{1,0:T(8,128)S(1)}, u32[]{:S(2)}, u32[]{:S(2)}) collective-permute-start(f32[310,128]{1,0:T(8,128)S(1)} %add.41), channel_id=1, source_target_pairs={{0,8},{4,12},{8,0},{12,4},{1,9},{5,13},{9,1},{13,5},{2,10},{6,14},... | collective-permute-start | bytes 476168 | tf_op jit(solution)/shard_map/ppermute | solution.py:242
  171.6 0.6 copy-start.10
  171.6 0.7 copy-start.11
  211.1 1.2 collective-permute-start.16

commit v3 on v2

--- a/solution.py
+++ b/solution.py
@@ -1,3 +1,4 @@
+import functools
 import math
 
 import jax
@@ -15,7 +16,7 @@
 OFF = 8
 ROWS_OUT = 8
 COLS_OUT = 32
-CELL_ROWS = 2
+CELL_ROWS = 4
 F32 = jnp.float32
 BF16 = jnp.bfloat16
 
@@ -71,7 +72,7 @@
 
 
 def cells_kernel(
-    tile, south, north, west, east, cot, mask, taps, bias, gain, shift, w_in, w_in_t, b_in, w_out_t,
+    tile, south, north, west, east, cot, mask, taps, bias, gain, shift, w_in, b_in, w_out,
     dy, g_in, g_out, g_chan, g_bin,
     ext, y, s_chan, s_bin,
 ):
@@ -108,13 +109,18 @@
         g_out[...] += lax.dot_general(
             act.astype(BF16), og, (((0,), (0,)), ((), ())), preferred_element_type=F32
         )
-        dpre = jnp.dot(og, w_out_t[...], preferred_element_type=F32) * slope
+        dact = lax.dot_general(
+            og, w_out[...], (((1,), (1,)), ((), ())), preferred_element_type=F32
+        )
+        dpre = dact * slope
         dpre_b = dpre.astype(BF16)
         s_bin[...] += partial_sum(dpre)
         g_in[...] += lax.dot_general(
             normed, dpre_b, (((0,), (0,)), ((), ())), preferred_element_type=F32
         )
-        dnorm = jnp.dot(dpre_b, w_in_t[...], preferred_element_type=F32)
+        dnorm = lax.dot_general(
+            dpre_b, w_in[...], (((1,), (1,)), ((), ())), preferred_element_type=F32
+        )
         s_chan[0] += partial_sum(dnorm * nhat)
         s_chan[1] += partial_sum(dnorm)
         dn = dnorm * gain[...]
@@ -131,7 +137,7 @@
     g_bin[...] = jnp.sum(s_bin[...], axis=0, keepdims=True)
 
 
-def taps_kernel(tile, south, north, west, east, dy, g_taps, ext, dyf):
+def taps_kernel(first, last, tile, south, north, west, east, dy, g_taps, ext, dyf):
     rows, cols, chans = tile.shape
     load_extended(ext, tile, south, north, west, east)
     edge = jnp.zeros((cols, chans), F32)
@@ -144,28 +150,26 @@
         return carry
 
     lax.fori_loop(0, rows, fill, 0)
-    for first, last in ((0, 4), (4, KS)):
-
-        def row_step(rho, acc):
-            def col_step(j, acc):
-                acc = list(acc)
-                for sub in range(8):
-                    c0 = pl.multiple_of(j * 64 + sub * 8, 8)
-                    d = [dyf[rho + (KS - 1) - a, pl.ds(c0, 8), :] for a in range(first, last)]
-                    for b in range(KS):
-                        v = ext[rho, pl.ds(c0 + (OFF - HALF + b), 8), :]
-                        for q in range(last - first):
-                            at = q * KS + b
-                            acc[at] = acc[at] + v * d[q]
-                return tuple(acc)
-
-            return lax.fori_loop(0, cols // 64, col_step, acc)
-
-        zero = jnp.zeros((8, chans), F32)
-        acc = lax.fori_loop(0, rows + KS - 1, row_step, (zero,) * (KS * (last - first)))
-        for n, value in enumerate(acc):
-            at = first * KS + n
-            g_taps[at : at + 1, :] = jnp.sum(value, axis=0, keepdims=True)
+
+    def row_step(rho, acc):
+        def col_step(j, acc):
+            acc = list(acc)
+            for sub in range(8):
+                c0 = pl.multiple_of(j * 64 + sub * 8, 8)
+                d = [dyf[rho + (KS - 1) - a, pl.ds(c0, 8), :] for a in range(first, last)]
+                for b in range(KS):
+                    v = ext[rho, pl.ds(c0 + (OFF - HALF + b), 8), :]
+                    for q in range(last - first):
+                        at = q * KS + b
+                        acc[at] = acc[at] + v * d[q]
+            return tuple(acc)
+
+        return lax.fori_loop(0, cols // 64, col_step, acc)
+
+    zero = jnp.zeros((8, chans), F32)
+    acc = lax.fori_loop(0, rows + KS - 1, row_step, (zero,) * (KS * (last - first)))
+    for n, value in enumerate(acc):
+        g_taps[n : n + 1, :] = jnp.sum(value, axis=0, keepdims=True)
 
 
 def input_kernel(tile, south, north, west, east, cot, taps, is_north, out, ext, fold, total):
@@ -202,21 +206,40 @@
     lax.fori_loop(0, cols // COLS_OUT, fold_step, 0)
 
 
-def halo(tile):
-    rows, cols, _ = tile.shape
+def row_halo(tile):
+    rows = tile.shape[0]
     lats, lons = lax.axis_size("lat"), lax.axis_size("lon")
-    up = [(i, i + 1) for i in range(lats - 1)]
-    down = [(i + 1, i) for i in range(lats - 1)]
-    south = lax.ppermute(tile[rows - HALF :], "lat", up)
-    above = lax.ppermute(tile[:HALF], "lat", down)
-    mirror = lax.ppermute(tile[rows - HALF :], "lon", [(i, lons - 1 - i) for i in range(lons)])
-    northern = lax.axis_index("lat") == lats - 1
-    north = jnp.where(northern, mirror[::-1, ::-1, :], above)
+    low, high = tile[:HALF], tile[rows - HALF :]
+    lat = lax.axis_index("lat")
+    if lats % 2:
+        south = lax.ppermute(high, "lat", [(i, i + 1) for i in range(lats - 1)])
+        above = lax.ppermute(low, "lat", [(i + 1, i) for i in range(lats - 1)])
+        mirror = lax.ppermute(high, "lon", [(i, lons - 1 - i) for i in range(lons)])
+        north = jnp.where(lat == lats - 1, mirror[::-1, ::-1, :], above)
+    else:
+        odd = lat % 2 == 1
+        first = lax.ppermute(jnp.where(odd, low, high), "lat", [(i, i ^ 1) for i in range(lats)])
+        route = []
+        for j in range(lons):
+            mirrored = lons - 1 - j
+            route.append((j * lats + lats - 1, mirrored * lats + lats - 1))
+            for i in range(1, lats - 1, 2):
+                route.append((j * lats + i, j * lats + i + 1))
+                route.append((j * lats + i + 1, j * lats + i))
+        second = lax.ppermute(jnp.where(odd, high, low), ("lon", "lat"), route)
+        folded = jnp.where(lat == lats - 1, second[::-1, ::-1, :], second)
+        south = jnp.where(odd, first, second)
+        north = jnp.where(odd, folded, first)
+    return south, north
+
+
+def column_halo(tile, south, north):
+    cols, lons = tile.shape[1], lax.axis_size("lon")
     left = jnp.concatenate([south[:, :HALF], tile[:, :HALF], north[:, :HALF]], 0)
     right = jnp.concatenate([south[:, cols - HALF :], tile[:, cols - HALF :], north[:, cols - HALF :]], 0)
     west = lax.ppermute(right, "lon", [(i, (i + 1) % lons) for i in range(lons)])
     east = lax.ppermute(left, "lon", [((i + 1) % lons, i) for i in range(lons)])
-    return south, north, west, east
+    return west, east
 
 
 def call(kernel, out_shape, scratch, flops, *args, scalars=0):
@@ -266,10 +289,13 @@
     northern = lax.axis_index("lat") == lax.axis_size("lat") - 1
     is_north = jnp.where(northern, 1.0, 0.0).astype(F32).reshape(1)
     work = 2 * KS * KS * rows * cols * chans * 128
+    in_share = chans // lax.axis_size("dp")
+    out_share = hidden // lax.axis_size("dp")
     sums, grads = None, []
     for n in range(batch):
         tile, cot = inputs[n], cotangent[n]
-        frame = halo(tile)
+        edge = row_halo(tile)
+        frame = (*edge, *column_halo(tile, *edge))
         dy, g_in, g_out, g_chan, g_bin = call(
             cells_kernel,
             (
@@ -287,15 +313,28 @@
             ],
             work,
             tile, *frame, cot, mask, taps, bias_dw[None], gain[None], shift_ln[None],
-            w_in, w_in.T, b_in[None], w_out.T,
-        )
-        g_taps = call(
-            taps_kernel,
-            shape((KS * KS, chans), F32),
-            [ext_shape, pltpu.VMEM((rows + 2 * (KS - 1), cols, chans), F32)],
-            work,
-            tile, *frame, dy,
-        )
+            w_in, b_in[None], w_out,
+        )
+        halves = (
+            dp_share(g_in, in_share).reshape(-1, chans),
+            dp_share(g_out, out_share),
+            axis_sum(jnp.concatenate([g_chan, g_bin.reshape(-1, chans)], 0), "dp"),
+        )
+
+        def taps_call(first, last, dy):
+            return call(
+                functools.partial(taps_kernel, first, last),
+                shape((KS * (last - first), chans), F32),
+                [ext_shape, pltpu.VMEM((rows + 2 * (KS - 1), cols, chans), F32)],
+                work // 2,
+                tile, *frame, dy,
+            )
+
+        taps_low = taps_call(0, 4, dy)
+        dy, south, north, *halves = lax.optimization_barrier((dy, *row_halo(dy), *halves))
+        strips = column_halo(dy, south, north)
+        cell_sum = axis_sum(jnp.concatenate(halves, 0), "lat")
+        g_taps = jnp.concatenate([taps_low, taps_call(4, KS, dy)], 0)
         grads.append(
             call(
                 input_kernel,
@@ -306,29 +345,19 @@
                     pltpu.VMEM((HALF, cols, chans), F32),
                 ],
                 work,
-                dy, *halo(dy), cot, taps, is_north, scalars=1,
+                dy, south, north, *strips, cot, taps, is_north, scalars=1,
             )
         )
-        own = (g_in, g_out, g_taps, g_chan, g_bin)
+        own = (cell_sum, g_taps)
         sums = own if sums is None else tuple(s + o for s, o in zip(sums, own))
-    g_in, g_out, g_taps, g_chan, g_bin = sums
+    total = axis_sum(jnp.concatenate(sums, 0), "lon")
     cells_all = lax.axis_size("dp") * batch * lax.axis_size("lat") * rows * lax.axis_size("lon") * cols
     scale = 1.0 / math.sqrt(cells_all)
-    in_share = chans // lax.axis_size("dp")
-    out_share = hidden // lax.axis_size("dp")
-    halves = (
-        dp_share(g_in, in_share).reshape(-1, chans),
-        dp_share(g_out, out_share),
-        axis_sum(jnp.concatenate([g_chan, g_bin.reshape(-1, chans)], 0), "dp"),
-    )
-    total = jnp.concatenate([*halves, g_taps], 0)
-    for axis in ("lat", "lon"):
-        total = axis_sum(total, axis)
     in_rows = in_share * hidden // chans
     parts = jnp.split(total, (in_rows, in_rows + out_share, in_rows + out_share + 3, total.shape[0] - KS * KS))
     s_in, s_out, s_chan, s_bin, s_taps = parts
     s_in, s_bin = s_in.reshape(in_share, hidden), s_bin.reshape(1, hidden)
-    s_taps = axis_sum(s_taps, "dp")
+    s_taps = axis_sum(axis_sum(s_taps, "dp"), "lat")
     return (
         jnp.stack(grads),
         s_in * scale,

time: 214 us -> 204 us (0.953)
  waiting for transfers between devices: 16.8 us -> 11.5 us
  local copies, waits for them, and re-layouts: 13.8 us -> 8.57 us
    ppermute x10 -> x8, waiting for transfers between devices: 9.87 us -> 6.6 us  [the longest x2 3.34 us: row_halo(): lax.ppermute(jnp.where(odd, low, high), 'lat', [(i, i ^ 1) for i in range...]
    unnamed x26 -> x28, local copies, waits for them, and re-layouts: 3.83 us -> 0.7 us
    pallas_call x3 -> x4, Pallas kernels: 151 us -> 149 us  [call(): pl.pallas_call(kernel, out_shape=out_shape, in_specs=[vmem] * (len(args)...]
    ppermute x5 -> x6, waiting for transfers between devices: 6.94 us -> 4.92 us  [axis_sum(): x = x + lax.ppermute(x, axis, [(i, i ^ step) for i in range(count)])]
    ppermute x5 -> x6, starting transfers between devices: 3.91 us -> 5.14 us  [axis_sum(): x = x + lax.ppermute(x, axis, [(i, i ^ step) for i in range(count)])]
    ppermute x10 -> x8, starting transfers between devices: 20.4 us -> 20.3 us  [the longest x2 13.9 us: row_halo(): lax.ppermute(jnp.where(odd, low, high), 'lat', [(i, i ^ 1) for i in range...]
  transfers between devices with their start and end apart: 17 -> 16, of which waited for: 4 -> 7; matrix products, arithmetic and copies ran while one was open for 5% -> 5% of each run, Pallas kernels for 37% -> 42%
where the time goes in v3:
time: 204 us; the launch traced here: 203 us
  Pallas kernels  149 us (73%)
  starting transfers between devices  26 us (13%)
  waiting for transfers between devices  11.5 us (6%)
  local copies, waits for them, and re-layouts  8.57 us (4%)
  other arithmetic  7.04 us (3%)
    pallas_call x4, Pallas kernels, call(): pl.pallas_call(kernel, out_shape=out_shape, in_specs=[vmem] * (len(args)...  149 us
    ppermute x2, starting transfers between devices, row_halo(): lax.ppermute(jnp.where(odd, low, high), 'lat', [(i, i ^ 1) for i in range...  13.9 us
    ppermute x6, starting transfers between devices, axis_sum(): x = x + lax.ppermute(x, axis, [(i, i ^ step) for i in range(count)])  5.14 us
    ppermute x6, waiting for transfers between devices, axis_sum(): x = x + lax.ppermute(x, axis, [(i, i ^ step) for i in range(count)])  4.92 us
  transfers between devices with their start and end apart: 16, of which 7 were waited for; matrix products, arithmetic and copies ran while one was open for 5% of the time, Pallas kernels for 42%

profile of v3, /device:TPU:0, one launch (start us, length us, event | category | flops | bytes accessed | tf_op | source)
XLA Modules:
  0.0 203.0 jit_solution(9147302228534503197)
XLA Ops:
  0.6 1.1 select_bitcast_fusion
  1.7 0.7 collective-permute-start.1
  2.4 7.8 %collective-permute-start = (bf16[3,256,128]{2,1,0:T(8,128)(2,1)S(1)}, bf16[3,256,128]{2,1,0:T(8,128)(2,1)S(1)}, u32[]{:S(2)}, u32[]{:S(2)}) collective-permute-start(bf16[3,256,128]{2,1,0:T(8,128)(2,1)S(1)} %get-tuple-element.37), channel_id=1, source_target_pairs={{0,2},{2,0},{1,3},{3,1},{4,6},{6,4},{5,7},{7,5},{8,10},{10,8},{9,1... | collective-permute-start | bytes 589832 | tf_op jit(solution)/shard_map/ppermute | solution.py:221
  10.2 1.0 fusion.6
  11.3 0.2 rev.6
  11.5 3.3 %collective-permute-done = bf16[3,256,128]{2,1,0:T(8,128)(2,1)S(1)} collective-permute-done((bf16[3,256,128]{2,1,0:T(8,128)(2,1)S(1)}, bf16[3,256,128]{2,1,0:T(8,128)(2,1)S(1)}, u32[]{:S(2)}, u32[]{:S(2)}) %collective-permute-start) | collective-permute-done | bytes 196640 | tf_op jit(solution)/shard_map/ppermute | solution.py:221
  15.0 0.3 collective-permute-start.3
  15.4 1.8 collective-permute-start.2
  17.2 0.7 convert_bitcast_fusion
  17.8 0.7 reshape.54
  18.6 0.1 broadcast_in_dim.30
  18.6 0.1 convert_element_type.10
  18.7 1.4 collective-permute-done.3.east
  20.1 1.4 collective-permute-done.2.west
  21.6 0.7 broadcast_in_dim.34.taps
  22.3 0.7 broadcast_in_dim.31.mask
  23.1 62.8 %shard_map.161 = (bf16[64,256,128]{2,1,0:T(8,128)(2,1)}, f32[128,256]{1,0:T(8,128)}, f32[256,128]{1,0:T(8,128)}, f32[3,128]{1,0:T(4,128)}, f32[1,256]{1,0:T(1,128)}) custom-call(bf16[64,256,128]{2,1,0:T(8,128)(2,1)} %bitcast.24, bf16[3,256,128]{2,1,0:T(8,128)(2,1)} %copy-done.1, bf16[3,256,128]{2,1,0:T(8,128)(2,1)} %copy-done, ...), custom_call_target="tpu_custom_call" | custom-call | flops 26306674688 | bytes 12582912 | tf_op jit(solution)/shard_map/pallas_call | solution.py:248
  85.9 0.7 pad_maximum_fusion.5
  86.6 0.9 constant_dynamic-slice_fusion
  87.4 0.5 collective-permute-start.7
  87.9 0.8 constant_dynamic-slice_fusion.1
  88.8 1.1 broadcast_select_fusion.1
  89.8 0.7 collective-permute-start.5
  90.6 6.0 %collective-permute-start.4 = (bf16[3,256,128]{2,1,0:T(8,128)(2,1)S(1)}, bf16[3,256,128]{2,1,0:T(8,128)(2,1)S(1)}, u32[]{:S(2)}, u32[]{:S(2)}) collective-permute-start(bf16[3,256,128]{2,1,0:T(8,128)(2,1)S(1)} %get-tuple-element.33), channel_id=1, source_target_pairs={{0,2},{2,0},{1,3},{3,1},{4,6},{6,4},{5,7},{7,5},{8,10},{10,8},{9,1... | collective-permute-start | bytes 589832 | tf_op jit(solution)/shard_map/ppermute | solution.py:221
  96.6 26.5 %shard_map.163 = f32[28,128]{1,0:T(8,128)} custom-call(bf16[64,256,128]{2,1,0:T(8,128)(2,1)} %bitcast.25, bf16[3,256,128]{2,1,0:T(8,128)(2,1)} %copy-done.1, bf16[3,256,128]{2,1,0:T(8,128)(2,1)} %copy-done, bf16[70,3,128]{2,1,0:T(4,128)(2,1)} %copy-done.10, bf16[70,3,128]{2,1,0:T(4,128)(2,1)} %copy-done.9, bf16[64,256,128]{2,1,0:T(8,128)(2,1)} %get-tuple-element.24.tile.dy), custom_call_target="tpu_custom_call" | custom-call | flops 13153337344 | bytes 12582912 | tf_op jit(solution)/shard_map/pallas_call | solution.py:248
  123.2 0.2 rev.7
  123.6 0.1 collective-permute-start.11
  123.7 1.0 fusion.5
  124.7 21.9 %shard_map.164 = f32[21,128]{1,0:T(8,128)} custom-call(bf16[64,256,128]{2,1,0:T(8,128)(2,1)} %bitcast.26, bf16[3,256,128]{2,1,0:T(8,128)(2,1)} %copy-done.1, bf16[3,256,128]{2,1,0:T(8,128)(2,1)} %copy-done, bf16[70,3,128]{2,1,0:T(4,128)(2,1)} %copy-done.10, bf16[70,3,128]{2,1,0:T(4,128)(2,1)} %copy-done.9, bf16[64,256,128]{2,1,0:T(8,128)(2,1)} %get-tuple-element.24.tile.dy), custom_call_target="tpu_custom_call" | custom-call | flops 13153337344 | bytes 12582912 | tf_op jit(solution)/shard_map/pallas_call | solution.py:248
  146.7 0.7 pad_maximum_fusion
  147.4 0.1 collective-permute-start.12
  147.6 2.9 %collective-permute-start.10 = (bf16[70,3,128]{2,1,0:T(4,128)(2,1)S(1)}, bf16[70,3,128]{2,1,0:T(4,128)(2,1)S(1)}, u32[]{:S(2)}, u32[]{:S(2)}) collective-permute-start(bf16[70,3,128]{2,1,0:T(4,128)(2,1)S(1)} %pad_maximum_fusion.4), channel_id=1, source_target_pairs={{4,0},{8,4},{12,8},{0,12},{5,1},{9,5},{13,9},{1,13},{6,2},{10,6},{... | collective-permute-start | bytes 161288 | tf_op jit(solution)/shard_map/ppermute | solution.py:241
  150.6 0.1 collective-permute-start.9
  150.6 3.6 %collective-permute-done.12 = f32[310,128]{1,0:T(8,128)S(1)} collective-permute-done((f32[310,128]{1,0:T(8,128)S(1)}, f32[310,128]{1,0:T(8,128)S(1)}, u32[]{:S(2)}, u32[]{:S(2)}) %collective-permute-start.12) | collective-permute-done | bytes 158752 | tf_op jit(solution)/shard_map/ppermute | solution.py:265
  154.2 0.7 fusion.11
  155.0 2.6 %collective-permute-start.13 = (f32[310,128]{1,0:T(8,128)S(1)}, f32[310,128]{1,0:T(8,128)S(1)}, u32[]{:S(2)}, u32[]{:S(2)}) collective-permute-start(f32[310,128]{1,0:T(8,128)S(1)} %fusion.11), channel_id=1, source_target_pairs={{0,8},{4,12},{8,0},{12,4},{1,9},{5,13},{9,1},{13,5},{2,10},{6,14},... | collective-permute-start | bytes 476168 | tf_op jit(solution)/shard_map/ppermute | solution.py:265
  157.5 0.4 collective-permute-done.9.west
  157.9 0.2 copy-done.11
  158.1 0.4 copy-done.12
  158.5 37.7 %shard_map.162 = bf16[64,256,128]{2,1,0:T(8,128)(2,1)} custom-call(bf16[64,256,128]{2,1,0:T(8,128)(2,1)} %get-tuple-element.24.tile.dy, bf16[3,256,128]{2,1,0:T(8,128)(2,1)} %copy-done.3, bf16[3,256,128]{2,1,0:T(8,128)(2,1)} %copy-done.2, bf16[70,3,128]{2,1,0:T(4,128)(2,1)} %copy-done.12, bf16[70,3,128]{2,1,0:T(4,128)(2,1)} %copy-done.11, ...), custom_call_target="tpu_custom_call" | custom-call | flops 26306674688 | bytes 12582912 | tf_op jit(solution)/shard_map/pallas_call | solution.py:248
  196.3 0.6 slice_multiply_fusion
  196.9 0.5 fusion.1
  197.5 0.7 collective-permute-done.14
  198.1 2.4 %collective-permute-start.15 = (f32[49,128]{1,0:T(8,128)S(1)}, f32[49,128]{1,0:T(8,128)S(1)}, u32[]{:S(2)}, u32[]{:S(2)}) collective-permute-start(f32[49,128]{1,0:T(8,128)S(1)} %slice_add_fusion), channel_id=1, source_target_pairs={{0,2},{2,0},{1,3},{3,1},{4,6},{6,4},{5,7},{7,5},{8,10},{10,8},{9,1... | collective-permute-start | bytes 75272 | tf_op jit(solution)/shard_map/ppermute | solution.py:265
  200.5 0.6 fusion
  201.1 0.6 mul.67
  201.8 0.6 collective-permute-done.15
  202.4 0.6 mul.71
  (57 shorter events, 0.5 us)
Async XLA Ops:
  1.7 9.6 %collective-permute-start.1 = (bf16[3,256,128]{2,1,0:T(8,128)(2,1)S(1)}, bf16[3,256,128]{2,1,0:T(8,128)(2,1)S(1)}, u32[]{:S(2)}, u32[]{:S(2)}) collective-permute-start(bf16[3,256,128]{2,1,0:T(8,128)(2,1)S(1)} %get-tuple-element.36), channel_id=1, source_target_pairs={{2,14},{6,10},{10,6},{14,2},{3,15},{7,11},{11,7},{15,3},{18,30},{2... | collective-permute-start | bytes 589832 | tf_op jit(solution)/shard_map/ppermute | solution.py:229
  2.4 12.5 %collective-permute-start = (bf16[3,256,128]{2,1,0:T(8,128)(2,1)S(1)}, bf16[3,256,128]{2,1,0:T(8,128)(2,1)S(1)}, u32[]{:S(2)}, u32[]{:S(2)}) collective-permute-start(bf16[3,256,128]{2,1,0:T(8,128)(2,1)S(1)} %get-tuple-element.37), channel_id=1, source_target_pairs={{0,2},{2,0},{1,3},{3,1},{4,6},{6,4},{5,7},{7,5},{8,10},{10,8},{9,1... | collective-permute-start | bytes 589832 | tf_op jit(solution)/shard_map/ppermute | solution.py:221
  14.9 8.2 %copy-start = (bf16[3,256,128]{2,1,0:T(8,128)(2,1)}, bf16[3,256,128]{2,1,0:T(8,128)(2,1)S(1)}, u32[]{:S(2)}) copy-start(bf16[3,256,128]{2,1,0:T(8,128)(2,1)S(1)} %get-tuple-element.40.north) | copy-start | bytes 589828
  14.9 8.2 %copy-start.1 = (bf16[3,256,128]{2,1,0:T(8,128)(2,1)}, bf16[3,256,128]{2,1,0:T(8,128)(2,1)S(1)}, u32[]{:S(2)}) copy-start(bf16[3,256,128]{2,1,0:T(8,128)(2,1)S(1)} %get-tuple-element.41.south) | copy-start | bytes 589828
  15.0 5.1 %collective-permute-start.3 = (bf16[70,3,128]{2,1,0:T(4,128)(2,1)S(1)}, bf16[70,3,128]{2,1,0:T(4,128)(2,1)S(1)}, u32[]{:S(2)}, u32[]{:S(2)}) collective-permute-start(bf16[70,3,128]{2,1,0:T(4,128)(2,1)S(1)} %pad_maximum_fusion.2), channel_id=1, source_target_pairs={{4,0},{8,4},{12,8},{0,12},{5,1},{9,5},{13,9},{1,13},{6,2},{10,6},{... | collective-permute-start | bytes 161288 | tf_op jit(solution)/shard_map/ppermute | solution.py:241
  15.4 6.2 %collective-permute-start.2 = (bf16[70,3,128]{2,1,0:T(4,128)(2,1)S(1)}, bf16[70,3,128]{2,1,0:T(4,128)(2,1)S(1)}, u32[]{:S(2)}, u32[]{:S(2)}) collective-permute-start(bf16[70,3,128]{2,1,0:T(4,128)(2,1)S(1)} %pad_maximum_fusion.1), channel_id=1, source_target_pairs={{0,4},{4,8},{8,12},{12,0},{1,5},{5,9},{9,13},{13,1},{2,6},{6,10},{... | collective-permute-start | bytes 161288 | tf_op jit(solution)/shard_map/ppermute | solution.py:240
  20.1 2.9 %copy-start.9 = (bf16[70,3,128]{2,1,0:T(4,128)(2,1)}, bf16[70,3,128]{2,1,0:T(4,128)(2,1)S(1)}, u32[]{:S(2)}) copy-start(bf16[70,3,128]{2,1,0:T(4,128)(2,1)S(1)} %collective-permute-done.3.east) | copy-start | bytes 161284
  21.6 1.5 copy-start.10
  86.6 36.5 %collective-permute-start.8 = (f32[5,128]{1,0:T(8,128)S(1)}, f32[5,128]{1,0:T(8,128)S(1)}, u32[]{:S(2)}, u32[]{:S(2)}) collective-permute-start(f32[5,128]{1,0:T(8,128)S(1)} %pad_maximum_fusion.5), channel_id=1, source_target_pairs={{0,1},{1,0},{2,3},{3,2},{4,5},{5,4},{6,7},{7,6},{8,9},{9,8},{10,11... | collective-permute-start | bytes 7688 | tf_op jit(solution)/shard_map/ppermute | solution.py:265
  87.4 35.7 %collective-permute-start.7 = (f32[128,128]{1,0:T(8,128)S(1)}, f32[128,128]{1,0:T(8,128)S(1)}, u32[]{:S(2)}, u32[]{:S(2)}) collective-permute-start(f32[128,128]{1,0:T(8,128)S(1)} %constant_dynamic-slice_fusion), channel_id=1, source_target_pairs={{0,1},{1,0},{2,3},{3,2},{4,5},{5,4},{6,7},{7,6},{8,9},{9,8},{10,11... | collective-permute-start | bytes 196616 | tf_op jit(solution)/shard_map/ppermute | solution.py:276
  88.8 34.3 %collective-permute-start.6 = (f32[64,256]{1,0:T(8,128)S(1)}, f32[64,256]{1,0:T(8,128)S(1)}, u32[]{:S(2)}, u32[]{:S(2)}) collective-permute-start(f32[64,256]{1,0:T(8,128)S(1)} %constant_dynamic-slice_fusion.1), channel_id=1, source_target_pairs={{0,1},{1,0},{2,3},{3,2},{4,5},{5,4},{6,7},{7,6},{8,9},{9,8},{10,11... | collective-permute-start | bytes 196616 | tf_op jit(solution)/shard_map/ppermute | solution.py:276
  89.8 33.4 %collective-permute-start.5 = (bf16[3,256,128]{2,1,0:T(8,128)(2,1)S(1)}, bf16[3,256,128]{2,1,0:T(8,128)(2,1)S(1)}, u32[]{:S(2)}, u32[]{:S(2)}) collective-permute-start(bf16[3,256,128]{2,1,0:T(8,128)(2,1)S(1)} %get-tuple-element.32), channel_id=1, source_target_pairs={{2,14},{6,10},{10,6},{14,2},{3,15},{7,11},{11,7},{15,3},{18,30},{2... | collective-permute-start | bytes 589832 | tf_op jit(solution)/shard_map/ppermute | solution.py:229
  90.5 32.6 %copy-start.7 = (f32[3,128]{1,0:T(4,128)S(1)}, f32[3,128]{1,0:T(4,128)}, u32[]{:S(2)}) copy-start(f32[3,128]{1,0:T(4,128)} %get-tuple-element.22) | copy-start | bytes 4612
  90.5 32.5 %copy-start.8 = (f32[1,256]{1,0:T(1,128)S(1)}, f32[1,256]{1,0:T(1,128)}, u32[]{:S(2)}) copy-start(f32[1,256]{1,0:T(1,128)} %get-tuple-element.23) | copy-start | bytes 3076
  90.5 32.6 %copy-start.5 = (f32[128,256]{1,0:T(8,128)S(1)}, f32[128,256]{1,0:T(8,128)}, u32[]{:S(2)}) copy-start(f32[128,256]{1,0:T(8,128)} %get-tuple-element.20) | copy-start | bytes 393220
  90.5 32.6 %copy-start.4 = (f32[256,128]{1,0:T(8,128)S(1)}, f32[256,128]{1,0:T(8,128)}, u32[]{:S(2)}) copy-start(f32[256,128]{1,0:T(8,128)} %get-tuple-element.21) | copy-start | bytes 393220
  90.6 32.9 %collective-permute-start.4 = (bf16[3,256,128]{2,1,0:T(8,128)(2,1)S(1)}, bf16[3,256,128]{2,1,0:T(8,128)(2,1)S(1)}, u32[]{:S(2)}, u32[]{:S(2)}) collective-permute-start(bf16[3,256,128]{2,1,0:T(8,128)(2,1)S(1)} %get-tuple-element.33), channel_id=1, source_target_pairs={{0,2},{2,0},{1,3},{3,1},{4,6},{6,4},{5,7},{7,5},{8,10},{10,8},{9,1... | collective-permute-start | bytes 589832 | tf_op jit(solution)/shard_map/ppermute | solution.py:221
  123.5 23.1 %copy-start.2 = (bf16[3,256,128]{2,1,0:T(8,128)(2,1)}, bf16[3,256,128]{2,1,0:T(8,128)(2,1)S(1)}, u32[]{:S(2)}) copy-start(bf16[3,256,128]{2,1,0:T(8,128)(2,1)S(1)} %get-tuple-element.26.north) | copy-start | bytes 589828
  123.5 23.1 %copy-start.3 = (bf16[3,256,128]{2,1,0:T(8,128)(2,1)}, bf16[3,256,128]{2,1,0:T(8,128)(2,1)S(1)}, u32[]{:S(2)}) copy-start(bf16[3,256,128]{2,1,0:T(8,128)(2,1)S(1)} %get-tuple-element.25.south) | copy-start | bytes 589828
  123.6 23.1 %collective-permute-start.11 = (f32[261,128]{1,0:T(8,128)S(1)}, f32[261,128]{1,0:T(8,128)S(1)}, u32[]{:S(2)}, u32[]{:S(2)}) collective-permute-start(f32[261,128]{1,0:T(8,128)S(1)} %constant_dynamic-update-slice_fusion), channel_id=1, source_target_pairs={{0,2},{2,0},{1,3},{3,1},{4,6},{6,4},{5,7},{7,5},{8,10},{10,8},{9,1... | collective-permute-start | bytes 400904 | tf_op jit(solution)/shard_map/ppermute | solution.py:265
  124.7 22.0 %copy-start.6 = (f32[28,128]{1,0:T(8,128)S(1)}, f32[28,128]{1,0:T(8,128)}, u32[]{:S(2)}) copy-start(f32[28,128]{1,0:T(8,128)} %shard_map.163) | copy-start | bytes 43012
  147.4 6.8 %collective-permute-start.12 = (f32[310,128]{1,0:T(8,128)S(1)}, f32[310,128]{1,0:T(8,128)S(1)}, u32[]{:S(2)}, u32[]{:S(2)}) collective-permute-start(f32[310,128]{1,0:T(8,128)S(1)} %pad_maximum_fusion), channel_id=1, source_target_pairs={{0,4},{4,0},{8,12},{12,8},{1,5},{5,1},{9,13},{13,9},{2,6},{6,2},{1... | collective-permute-start | bytes 476168 | tf_op jit(solution)/shard_map/ppermute | solution.py:265
  147.6 9.9 %collective-permute-start.10 = (bf16[70,3,128]{2,1,0:T(4,128)(2,1)S(1)}, bf16[70,3,128]{2,1,0:T(4,128)(2,1)S(1)}, u32[]{:S(2)}, u32[]{:S(2)}) collective-permute-start(bf16[70,3,128]{2,1,0:T(4,128)(2,1)S(1)} %pad_maximum_fusion.4), channel_id=1, source_target_pairs={{4,0},{8,4},{12,8},{0,12},{5,1},{9,5},{13,9},{1,13},{6,2},{10,6},{... | collective-permute-start | bytes 161288 | tf_op jit(solution)/shard_map/ppermute | solution.py:241
  150.6 7.4 %collective-permute-start.9 = (bf16[70,3,128]{2,1,0:T(4,128)(2,1)S(1)}, bf16[70,3,128]{2,1,0:T(4,128)(2,1)S(1)}, u32[]{:S(2)}, u32[]{:S(2)}) collective-permute-start(bf16[70,3,128]{2,1,0:T(4,128)(2,1)S(1)} %pad_maximum_fusion.3), channel_id=1, source_target_pairs={{0,4},{4,8},{8,12},{12,0},{1,5},{5,9},{9,13},{13,1},{2,6},{6,10},{... | collective-permute-start | bytes 161288 | tf_op jit(solution)/shard_map/ppermute | solution.py:240
  155.0 41.3 %collective-permute-start.13 = (f32[310,128]{1,0:T(8,128)S(1)}, f32[310,128]{1,0:T(8,128)S(1)}, u32[]{:S(2)}, u32[]{:S(2)}) collective-permute-start(f32[310,128]{1,0:T(8,128)S(1)} %fusion.11), channel_id=1, source_target_pairs={{0,8},{4,12},{8,0},{12,4},{1,9},{5,13},{9,1},{13,5},{2,10},{6,14},... | collective-permute-start | bytes 476168 | tf_op jit(solution)/shard_map/ppermute | solution.py:265
  157.5 0.6 copy-start.11
  157.9 0.6 copy-start.12
  196.9 1.2 collective-permute-start.14
  198.1 4.3 %collective-permute-start.15 = (f32[49,128]{1,0:T(8,128)S(1)}, f32[49,128]{1,0:T(8,128)S(1)}, u32[]{:S(2)}, u32[]{:S(2)}) collective-permute-start(f32[49,128]{1,0:T(8,128)S(1)} %slice_add_fusion), channel_id=1, source_target_pairs={{0,2},{2,0},{1,3},{3,1},{4,6},{6,4},{5,7},{7,5},{8,10},{10,8},{9,1... | collective-permute-start | bytes 75272 | tf_op jit(solution)/shard_map/ppermute | solution.py:265

commit v4 on v3

--- a/solution.py
+++ b/solution.py
@@ -16,7 +16,7 @@
 OFF = 8
 ROWS_OUT = 8
 COLS_OUT = 32
-CELL_ROWS = 4
+CELL_ROWS = 8
 F32 = jnp.float32
 BF16 = jnp.bfloat16
 

time: 204 us -> 200 us (0.980)
  Pallas kernels: 149 us -> 145 us
    pallas_call x4, Pallas kernels: 149 us -> 145 us  [call(): pl.pallas_call(kernel, out_shape=out_shape, in_specs=[vmem] * (len(args)...]
  transfers between devices with their start and end apart: 16 -> 16, of which waited for: 7 -> 7; matrix products, arithmetic and copies ran while one was open for 5% -> 5% of each run, Pallas kernels for 42% -> 43%
where the time goes in v4:
time: 200 us
  Pallas kernels  145 us (72%)
  starting transfers between devices  26 us (13%)
  waiting for transfers between devices  11.5 us (6%)
  local copies, waits for them, and re-layouts  8.57 us (4%)
  other arithmetic  7.04 us (4%)
    pallas_call x4, Pallas kernels, call(): pl.pallas_call(kernel, out_shape=out_shape, in_specs=[vmem] * (len(args)...  145 us
    ppermute x2, starting transfers between devices, row_halo(): lax.ppermute(jnp.where(odd, low, high), 'lat', [(i, i ^ 1) for i in range...  13.9 us
    ppermute x6, starting transfers between devices, axis_sum(): x = x + lax.ppermute(x, axis, [(i, i ^ step) for i in range(count)])  5.19 us
    ppermute x6, waiting for transfers between devices, axis_sum(): x = x + lax.ppermute(x, axis, [(i, i ^ step) for i in range(count)])  4.93 us
  transfers between devices with their start and end apart: 16, of which 7 were waited for; matrix products, arithmetic and copies ran while one was open for 5% of the time, Pallas kernels for 43%

profile of v4, /device:TPU:0, one launch (start us, length us, event | category | flops | bytes accessed | tf_op | source)
XLA Modules:
  0.0 199.6 jit_solution(4001531852596406896)
XLA Ops:
  0.6 1.1 select_bitcast_fusion
  1.7 0.7 collective-permute-start.1
  2.4 7.8 %collective-permute-start = (bf16[3,256,128]{2,1,0:T(8,128)(2,1)S(1)}, bf16[3,256,128]{2,1,0:T(8,128)(2,1)S(1)}, u32[]{:S(2)}, u32[]{:S(2)}) collective-permute-start(bf16[3,256,128]{2,1,0:T(8,128)(2,1)S(1)} %get-tuple-element.37), channel_id=1, source_target_pairs={{0,2},{2,0},{1,3},{3,1},{4,6},{6,4},{5,7},{7,5},{8,10},{10,8},{9,1... | collective-permute-start | bytes 589832 | tf_op jit(solution)/shard_map/ppermute | solution.py:221
  10.2 1.0 fusion.6
  11.3 0.2 rev.6
  11.5 3.3 %collective-permute-done = bf16[3,256,128]{2,1,0:T(8,128)(2,1)S(1)} collective-permute-done((bf16[3,256,128]{2,1,0:T(8,128)(2,1)S(1)}, bf16[3,256,128]{2,1,0:T(8,128)(2,1)S(1)}, u32[]{:S(2)}, u32[]{:S(2)}) %collective-permute-start) | collective-permute-done | bytes 196640 | tf_op jit(solution)/shard_map/ppermute | solution.py:221
  15.0 0.3 collective-permute-start.3
  15.4 1.8 collective-permute-start.2
  17.2 0.7 convert_bitcast_fusion
  17.8 0.7 reshape.54
  18.6 0.1 broadcast_in_dim.30
  18.6 0.1 convert_element_type.10
  18.7 1.4 collective-permute-done.3.east
  20.1 1.4 collective-permute-done.2.west
  21.6 0.7 broadcast_in_dim.34.taps
  22.3 0.7 broadcast_in_dim.31.mask
  23.1 59.3 %shard_map.161 = (bf16[64,256,128]{2,1,0:T(8,128)(2,1)}, f32[128,256]{1,0:T(8,128)}, f32[256,128]{1,0:T(8,128)}, f32[3,128]{1,0:T(4,128)}, f32[1,256]{1,0:T(1,128)}) custom-call(bf16[64,256,128]{2,1,0:T(8,128)(2,1)} %bitcast.24, bf16[3,256,128]{2,1,0:T(8,128)(2,1)} %copy-done.1, bf16[3,256,128]{2,1,0:T(8,128)(2,1)} %copy-done, ...), custom_call_target="tpu_custom_call" | custom-call | flops 26306674688 | bytes 12582912 | tf_op jit(solution)/shard_map/pallas_call | solution.py:248
  82.4 0.7 pad_maximum_fusion.5
  83.1 0.9 constant_dynamic-slice_fusion
  84.0 0.5 collective-permute-start.7
  84.5 0.8 constant_dynamic-slice_fusion.1
  85.3 1.1 broadcast_select_fusion.1
  86.4 0.7 collective-permute-start.5
  87.1 6.0 %collective-permute-start.4 = (bf16[3,256,128]{2,1,0:T(8,128)(2,1)S(1)}, bf16[3,256,128]{2,1,0:T(8,128)(2,1)S(1)}, u32[]{:S(2)}, u32[]{:S(2)}) collective-permute-start(bf16[3,256,128]{2,1,0:T(8,128)(2,1)S(1)} %get-tuple-element.33), channel_id=1, source_target_pairs={{0,2},{2,0},{1,3},{3,1},{4,6},{6,4},{5,7},{7,5},{8,10},{10,8},{9,1... | collective-permute-start | bytes 589832 | tf_op jit(solution)/shard_map/ppermute | solution.py:221
  93.1 26.5 %shard_map.163 = f32[28,128]{1,0:T(8,128)} custom-call(bf16[64,256,128]{2,1,0:T(8,128)(2,1)} %bitcast.25, bf16[3,256,128]{2,1,0:T(8,128)(2,1)} %copy-done.1, bf16[3,256,128]{2,1,0:T(8,128)(2,1)} %copy-done, bf16[70,3,128]{2,1,0:T(4,128)(2,1)} %copy-done.10, bf16[70,3,128]{2,1,0:T(4,128)(2,1)} %copy-done.9, bf16[64,256,128]{2,1,0:T(8,128)(2,1)} %get-tuple-element.24.tile.dy), custom_call_target="tpu_custom_call" | custom-call | flops 13153337344 | bytes 12582912 | tf_op jit(solution)/shard_map/pallas_call | solution.py:248
  119.7 0.2 rev.7
  120.1 0.1 collective-permute-start.11
  120.2 1.0 fusion.5
  121.3 21.9 %shard_map.164 = f32[21,128]{1,0:T(8,128)} custom-call(bf16[64,256,128]{2,1,0:T(8,128)(2,1)} %bitcast.26, bf16[3,256,128]{2,1,0:T(8,128)(2,1)} %copy-done.1, bf16[3,256,128]{2,1,0:T(8,128)(2,1)} %copy-done, bf16[70,3,128]{2,1,0:T(4,128)(2,1)} %copy-done.10, bf16[70,3,128]{2,1,0:T(4,128)(2,1)} %copy-done.9, bf16[64,256,128]{2,1,0:T(8,128)(2,1)} %get-tuple-element.24.tile.dy), custom_call_target="tpu_custom_call" | custom-call | flops 13153337344 | bytes 12582912 | tf_op jit(solution)/shard_map/pallas_call | solution.py:248
  143.2 0.7 pad_maximum_fusion
  144.0 0.1 collective-permute-start.12
  144.1 2.9 %collective-permute-start.10 = (bf16[70,3,128]{2,1,0:T(4,128)(2,1)S(1)}, bf16[70,3,128]{2,1,0:T(4,128)(2,1)S(1)}, u32[]{:S(2)}, u32[]{:S(2)}) collective-permute-start(bf16[70,3,128]{2,1,0:T(4,128)(2,1)S(1)} %pad_maximum_fusion.4), channel_id=1, source_target_pairs={{4,0},{8,4},{12,8},{0,12},{5,1},{9,5},{13,9},{1,13},{6,2},{10,6},{... | collective-permute-start | bytes 161288 | tf_op jit(solution)/shard_map/ppermute | solution.py:241
  147.1 0.1 collective-permute-start.9
  147.2 3.6 %collective-permute-done.12 = f32[310,128]{1,0:T(8,128)S(1)} collective-permute-done((f32[310,128]{1,0:T(8,128)S(1)}, f32[310,128]{1,0:T(8,128)S(1)}, u32[]{:S(2)}, u32[]{:S(2)}) %collective-permute-start.12) | collective-permute-done | bytes 158752 | tf_op jit(solution)/shard_map/ppermute | solution.py:265
  150.8 0.7 fusion.11
  151.5 2.5 %collective-permute-start.13 = (f32[310,128]{1,0:T(8,128)S(1)}, f32[310,128]{1,0:T(8,128)S(1)}, u32[]{:S(2)}, u32[]{:S(2)}) collective-permute-start(f32[310,128]{1,0:T(8,128)S(1)} %fusion.11), channel_id=1, source_target_pairs={{0,8},{4,12},{8,0},{12,4},{1,9},{5,13},{9,1},{13,5},{2,10},{6,14},... | collective-permute-start | bytes 476168 | tf_op jit(solution)/shard_map/ppermute | solution.py:265
  154.0 0.3 collective-permute-done.9.west
  154.4 0.3 copy-done.11
  154.7 0.3 copy-done.12
  155.0 37.7 %shard_map.162 = bf16[64,256,128]{2,1,0:T(8,128)(2,1)} custom-call(bf16[64,256,128]{2,1,0:T(8,128)(2,1)} %get-tuple-element.24.tile.dy, bf16[3,256,128]{2,1,0:T(8,128)(2,1)} %copy-done.3, bf16[3,256,128]{2,1,0:T(8,128)(2,1)} %copy-done.2, bf16[70,3,128]{2,1,0:T(4,128)(2,1)} %copy-done.12, bf16[70,3,128]{2,1,0:T(4,128)(2,1)} %copy-done.11, ...), custom_call_target="tpu_custom_call" | custom-call | flops 26306674688 | bytes 12582912 | tf_op jit(solution)/shard_map/pallas_call | solution.py:248
  192.8 0.6 slice_multiply_fusion
  193.4 0.5 fusion.1
  193.9 0.7 collective-permute-done.14
  194.6 2.5 %collective-permute-start.15 = (f32[49,128]{1,0:T(8,128)S(1)}, f32[49,128]{1,0:T(8,128)S(1)}, u32[]{:S(2)}, u32[]{:S(2)}) collective-permute-start(f32[49,128]{1,0:T(8,128)S(1)} %slice_add_fusion), channel_id=1, source_target_pairs={{0,2},{2,0},{1,3},{3,1},{4,6},{6,4},{5,7},{7,5},{8,10},{10,8},{9,1... | collective-permute-start | bytes 75272 | tf_op jit(solution)/shard_map/ppermute | solution.py:265
  197.1 0.6 fusion
  197.6 0.6 mul.67
  198.3 0.6 collective-permute-done.15
  198.9 0.6 mul.71
  (57 shorter events, 0.5 us)
Async XLA Ops:
  1.7 9.6 %collective-permute-start.1 = (bf16[3,256,128]{2,1,0:T(8,128)(2,1)S(1)}, bf16[3,256,128]{2,1,0:T(8,128)(2,1)S(1)}, u32[]{:S(2)}, u32[]{:S(2)}) collective-permute-start(bf16[3,256,128]{2,1,0:T(8,128)(2,1)S(1)} %get-tuple-element.36), channel_id=1, source_target_pairs={{2,14},{6,10},{10,6},{14,2},{3,15},{7,11},{11,7},{15,3},{18,30},{2... | collective-permute-start | bytes 589832 | tf_op jit(solution)/shard_map/ppermute | solution.py:229
  2.4 12.5 %collective-permute-start = (bf16[3,256,128]{2,1,0:T(8,128)(2,1)S(1)}, bf16[3,256,128]{2,1,0:T(8,128)(2,1)S(1)}, u32[]{:S(2)}, u32[]{:S(2)}) collective-permute-start(bf16[3,256,128]{2,1,0:T(8,128)(2,1)S(1)} %get-tuple-element.37), channel_id=1, source_target_pairs={{0,2},{2,0},{1,3},{3,1},{4,6},{6,4},{5,7},{7,5},{8,10},{10,8},{9,1... | collective-permute-start | bytes 589832 | tf_op jit(solution)/shard_map/ppermute | solution.py:221
  14.9 8.2 %copy-start = (bf16[3,256,128]{2,1,0:T(8,128)(2,1)}, bf16[3,256,128]{2,1,0:T(8,128)(2,1)S(1)}, u32[]{:S(2)}) copy-start(bf16[3,256,128]{2,1,0:T(8,128)(2,1)S(1)} %get-tuple-element.40.north) | copy-start | bytes 589828
  14.9 8.2 %copy-start.1 = (bf16[3,256,128]{2,1,0:T(8,128)(2,1)}, bf16[3,256,128]{2,1,0:T(8,128)(2,1)S(1)}, u32[]{:S(2)}) copy-start(bf16[3,256,128]{2,1,0:T(8,128)(2,1)S(1)} %get-tuple-element.41.south) | copy-start | bytes 589828
  15.0 5.1 %collective-permute-start.3 = (bf16[70,3,128]{2,1,0:T(4,128)(2,1)S(1)}, bf16[70,3,128]{2,1,0:T(4,128)(2,1)S(1)}, u32[]{:S(2)}, u32[]{:S(2)}) collective-permute-start(bf16[70,3,128]{2,1,0:T(4,128)(2,1)S(1)} %pad_maximum_fusion.2), channel_id=1, source_target_pairs={{4,0},{8,4},{12,8},{0,12},{5,1},{9,5},{13,9},{1,13},{6,2},{10,6},{... | collective-permute-start | bytes 161288 | tf_op jit(solution)/shard_map/ppermute | solution.py:241
  15.4 6.2 %collective-permute-start.2 = (bf16[70,3,128]{2,1,0:T(4,128)(2,1)S(1)}, bf16[70,3,128]{2,1,0:T(4,128)(2,1)S(1)}, u32[]{:S(2)}, u32[]{:S(2)}) collective-permute-start(bf16[70,3,128]{2,1,0:T(4,128)(2,1)S(1)} %pad_maximum_fusion.1), channel_id=1, source_target_pairs={{0,4},{4,8},{8,12},{12,0},{1,5},{5,9},{9,13},{13,1},{2,6},{6,10},{... | collective-permute-start | bytes 161288 | tf_op jit(solution)/shard_map/ppermute | solution.py:240
  20.1 2.9 %copy-start.9 = (bf16[70,3,128]{2,1,0:T(4,128)(2,1)}, bf16[70,3,128]{2,1,0:T(4,128)(2,1)S(1)}, u32[]{:S(2)}) copy-start(bf16[70,3,128]{2,1,0:T(4,128)(2,1)S(1)} %collective-permute-done.3.east) | copy-start | bytes 161284
  21.6 1.5 copy-start.10
  83.1 36.5 %collective-permute-start.8 = (f32[5,128]{1,0:T(8,128)S(1)}, f32[5,128]{1,0:T(8,128)S(1)}, u32[]{:S(2)}, u32[]{:S(2)}) collective-permute-start(f32[5,128]{1,0:T(8,128)S(1)} %pad_maximum_fusion.5), channel_id=1, source_target_pairs={{0,1},{1,0},{2,3},{3,2},{4,5},{5,4},{6,7},{7,6},{8,9},{9,8},{10,11... | collective-permute-start | bytes 7688 | tf_op jit(solution)/shard_map/ppermute | solution.py:265
  84.0 35.7 %collective-permute-start.7 = (f32[128,128]{1,0:T(8,128)S(1)}, f32[128,128]{1,0:T(8,128)S(1)}, u32[]{:S(2)}, u32[]{:S(2)}) collective-permute-start(f32[128,128]{1,0:T(8,128)S(1)} %constant_dynamic-slice_fusion), channel_id=1, source_target_pairs={{0,1},{1,0},{2,3},{3,2},{4,5},{5,4},{6,7},{7,6},{8,9},{9,8},{10,11... | collective-permute-start | bytes 196616 | tf_op jit(solution)/shard_map/ppermute | solution.py:276
  85.3 34.3 %collective-permute-start.6 = (f32[64,256]{1,0:T(8,128)S(1)}, f32[64,256]{1,0:T(8,128)S(1)}, u32[]{:S(2)}, u32[]{:S(2)}) collective-permute-start(f32[64,256]{1,0:T(8,128)S(1)} %constant_dynamic-slice_fusion.1), channel_id=1, source_target_pairs={{0,1},{1,0},{2,3},{3,2},{4,5},{5,4},{6,7},{7,6},{8,9},{9,8},{10,11... | collective-permute-start | bytes 196616 | tf_op jit(solution)/shard_map/ppermute | solution.py:276
  86.4 33.4 %collective-permute-start.5 = (bf16[3,256,128]{2,1,0:T(8,128)(2,1)S(1)}, bf16[3,256,128]{2,1,0:T(8,128)(2,1)S(1)}, u32[]{:S(2)}, u32[]{:S(2)}) collective-permute-start(bf16[3,256,128]{2,1,0:T(8,128)(2,1)S(1)} %get-tuple-element.32), channel_id=1, source_target_pairs={{2,14},{6,10},{10,6},{14,2},{3,15},{7,11},{11,7},{15,3},{18,30},{2... | collective-permute-start | bytes 589832 | tf_op jit(solution)/shard_map/ppermute | solution.py:229
  87.1 32.6 %copy-start.7 = (f32[3,128]{1,0:T(4,128)S(1)}, f32[3,128]{1,0:T(4,128)}, u32[]{:S(2)}) copy-start(f32[3,128]{1,0:T(4,128)} %get-tuple-element.22) | copy-start | bytes 4612
  87.1 32.5 %copy-start.8 = (f32[1,256]{1,0:T(1,128)S(1)}, f32[1,256]{1,0:T(1,128)}, u32[]{:S(2)}) copy-start(f32[1,256]{1,0:T(1,128)} %get-tuple-element.23) | copy-start | bytes 3076
  87.1 32.6 %copy-start.5 = (f32[128,256]{1,0:T(8,128)S(1)}, f32[128,256]{1,0:T(8,128)}, u32[]{:S(2)}) copy-start(f32[128,256]{1,0:T(8,128)} %get-tuple-element.20) | copy-start | bytes 393220
  87.1 32.6 %copy-start.4 = (f32[256,128]{1,0:T(8,128)S(1)}, f32[256,128]{1,0:T(8,128)}, u32[]{:S(2)}) copy-start(f32[256,128]{1,0:T(8,128)} %get-tuple-element.21) | copy-start | bytes 393220
  87.1 32.9 %collective-permute-start.4 = (bf16[3,256,128]{2,1,0:T(8,128)(2,1)S(1)}, bf16[3,256,128]{2,1,0:T(8,128)(2,1)S(1)}, u32[]{:S(2)}, u32[]{:S(2)}) collective-permute-start(bf16[3,256,128]{2,1,0:T(8,128)(2,1)S(1)} %get-tuple-element.33), channel_id=1, source_target_pairs={{0,2},{2,0},{1,3},{3,1},{4,6},{6,4},{5,7},{7,5},{8,10},{10,8},{9,1... | collective-permute-start | bytes 589832 | tf_op jit(solution)/shard_map/ppermute | solution.py:221
  120.0 23.1 %copy-start.2 = (bf16[3,256,128]{2,1,0:T(8,128)(2,1)}, bf16[3,256,128]{2,1,0:T(8,128)(2,1)S(1)}, u32[]{:S(2)}) copy-start(bf16[3,256,128]{2,1,0:T(8,128)(2,1)S(1)} %get-tuple-element.26.north) | copy-start | bytes 589828
  120.1 23.1 %copy-start.3 = (bf16[3,256,128]{2,1,0:T(8,128)(2,1)}, bf16[3,256,128]{2,1,0:T(8,128)(2,1)S(1)}, u32[]{:S(2)}) copy-start(bf16[3,256,128]{2,1,0:T(8,128)(2,1)S(1)} %get-tuple-element.25.south) | copy-start | bytes 589828
  120.1 23.1 %collective-permute-start.11 = (f32[261,128]{1,0:T(8,128)S(1)}, f32[261,128]{1,0:T(8,128)S(1)}, u32[]{:S(2)}, u32[]{:S(2)}) collective-permute-start(f32[261,128]{1,0:T(8,128)S(1)} %constant_dynamic-update-slice_fusion), channel_id=1, source_target_pairs={{0,2},{2,0},{1,3},{3,1},{4,6},{6,4},{5,7},{7,5},{8,10},{10,8},{9,1... | collective-permute-start | bytes 400904 | tf_op jit(solution)/shard_map/ppermute | solution.py:265
  121.3 22.0 %copy-start.6 = (f32[28,128]{1,0:T(8,128)S(1)}, f32[28,128]{1,0:T(8,128)}, u32[]{:S(2)}) copy-start(f32[28,128]{1,0:T(8,128)} %shard_map.163) | copy-start | bytes 43012
  144.0 6.8 %collective-permute-start.12 = (f32[310,128]{1,0:T(8,128)S(1)}, f32[310,128]{1,0:T(8,128)S(1)}, u32[]{:S(2)}, u32[]{:S(2)}) collective-permute-start(f32[310,128]{1,0:T(8,128)S(1)} %pad_maximum_fusion), channel_id=1, source_target_pairs={{0,4},{4,0},{8,12},{12,8},{1,5},{5,1},{9,13},{13,9},{2,6},{6,2},{1... | collective-permute-start | bytes 476168 | tf_op jit(solution)/shard_map/ppermute | solution.py:265
  144.1 9.9 %collective-permute-start.10 = (bf16[70,3,128]{2,1,0:T(4,128)(2,1)S(1)}, bf16[70,3,128]{2,1,0:T(4,128)(2,1)S(1)}, u32[]{:S(2)}, u32[]{:S(2)}) collective-permute-start(bf16[70,3,128]{2,1,0:T(4,128)(2,1)S(1)} %pad_maximum_fusion.4), channel_id=1, source_target_pairs={{4,0},{8,4},{12,8},{0,12},{5,1},{9,5},{13,9},{1,13},{6,2},{10,6},{... | collective-permute-start | bytes 161288 | tf_op jit(solution)/shard_map/ppermute | solution.py:241
  147.1 7.3 %collective-permute-start.9 = (bf16[70,3,128]{2,1,0:T(4,128)(2,1)S(1)}, bf16[70,3,128]{2,1,0:T(4,128)(2,1)S(1)}, u32[]{:S(2)}, u32[]{:S(2)}) collective-permute-start(bf16[70,3,128]{2,1,0:T(4,128)(2,1)S(1)} %pad_maximum_fusion.3), channel_id=1, source_target_pairs={{0,4},{4,8},{8,12},{12,0},{1,5},{5,9},{9,13},{13,1},{2,6},{6,10},{... | collective-permute-start | bytes 161288 | tf_op jit(solution)/shard_map/ppermute | solution.py:240
  151.5 41.2 %collective-permute-start.13 = (f32[310,128]{1,0:T(8,128)S(1)}, f32[310,128]{1,0:T(8,128)S(1)}, u32[]{:S(2)}, u32[]{:S(2)}) collective-permute-start(f32[310,128]{1,0:T(8,128)S(1)} %fusion.11), channel_id=1, source_target_pairs={{0,8},{4,12},{8,0},{12,4},{1,9},{5,13},{9,1},{13,5},{2,10},{6,14},... | collective-permute-start | bytes 476168 | tf_op jit(solution)/shard_map/ppermute | solution.py:265
  154.0 0.6 copy-start.11
  154.4 0.6 copy-start.12
  193.4 1.2 collective-permute-start.14
  194.6 4.3 %collective-permute-start.15 = (f32[49,128]{1,0:T(8,128)S(1)}, f32[49,128]{1,0:T(8,128)S(1)}, u32[]{:S(2)}, u32[]{:S(2)}) collective-permute-start(f32[49,128]{1,0:T(8,128)S(1)} %slice_add_fusion), channel_id=1, source_target_pairs={{0,2},{2,0},{1,3},{3,1},{4,6},{6,4},{5,7},{7,5},{8,10},{10,8},{9,1... | collective-permute-start | bytes 75272 | tf_op jit(solution)/shard_map/ppermute | solution.py:265
